TPU v7x, 256 devices: a whole 4x4x8 slice. The times are simulated.
256 devices in a mesh: tm: 16 (over z_hi, y), space: 16 (over x, z_lo, core).
Axes of the slice: x: 4, y: 4, z: 8 (z_hi: 4, z_lo: 2; z = z_hi * 2 + z_lo), core: 2. Of those that a mesh axis runs over, the one named last changes fastest.
Arguments:
- snapshots: bfloat16 [3, 4096, 16384], P(None, 'tm', 'space'), may hold values from -6 to 6
- tile_table: int32 [16, 20, 2], P('tm'), may hold values from -1 to 15, as said below
Outputs:
- gram_tiles: float32 [16, 20, 256, 256], P('tm', None, 'space')
Inputs may be any that keep to these rules, and one draw needn't show every extreme that they name: `tile_table`: every pair a <= b of block numbers below 16 stands in exactly one slot of the table, with a as row block and b as column block. In each owner's row the filled slots come first and the empty slots, -1 in both entries, last. Some owner has all 20 slots filled; owners may have no tiles.
All inputs are finite; a program needn't handle non-finite values.
Results may differ from a plain program's by a relative error of at most 0.0003.
Values may be sent and summed in bfloat16 or wider, within the bound.
A program may use at most 128 MiB of HBM per device.

v0:
```python
import math

import jax
import jax.numpy as jnp
from jax import lax
from jax.sharding import PartitionSpec as P


def pair_tile(left_block, right_block):
    return jnp.einsum("kic,kjc->ij", left_block, right_block, preferred_element_type=jnp.float32)


def per_device(snapshots, tile_table):
    block_size = snapshots.shape[1]
    cells_dev = snapshots.shape[2]
    space_count = lax.axis_size("space")
    scale_factor = 1.0 / math.sqrt(3 * cells_dev * space_count)
    table = tile_table[0]
    row_block = table[:, 0]
    col_block = table[:, 1]
    slot_count = table.shape[0]
    valid = row_block >= 0
    whole = lax.all_gather(snapshots, "tm", axis=1, tiled=True)
    filled = jnp.sum(valid.astype(jnp.int32))

    def add_tile(slot, stacked):
        first = jnp.maximum(row_block[slot], 0)
        second = jnp.maximum(col_block[slot], 0)
        left_block = lax.dynamic_slice_in_dim(whole, first * block_size, block_size, 1)
        right_block = lax.dynamic_slice_in_dim(whole, second * block_size, block_size, 1)
        product = pair_tile(left_block, right_block)
        return lax.dynamic_update_index_in_dim(stacked, product, slot, 0)

    empty = jnp.zeros((slot_count, block_size, block_size), jnp.float32)
    partial_tiles = lax.fori_loop(0, filled, add_tile, empty)
    summed = lax.psum_scatter(partial_tiles, "space", scatter_dimension=1, tiled=True)
    result = summed * scale_factor
    zeros_tile = jnp.zeros_like(result)
    result = jnp.where(valid[:, None, None], result, zeros_tile)
    return result[None]


def solution(mesh):
    in_specs = (P(None, "tm", "space"), P("tm", None, None))
    out_specs = P("tm", None, "space", None)
    return jax.shard_map(
        per_device, mesh=mesh, in_specs=in_specs, out_specs=out_specs, check_vma=False
    )
```

profile of v0, /device:TPU:16, one launch (start us, length us, event | category | flops | bytes accessed | tf_op | source)
XLA Modules:
  0.0 509.1 jit_solution(5449932151915418883)
XLA Ops:
  6.5 0.7 all-gather.2.cloned.1.call-update
  7.3 0.0 reduce-scatter.2.cloned.1.call-start
  7.3 1.4 convert_reduce_fusion
  8.7 0.8 slice_bitcast_fusion
  9.4 291.5 %all-gather.2.cloned.1.call-done = bf16[3,4096,1024]{2,1,0:T(8,128)(2,1)} async-done(((bf16[3,256,1024]{2,1,0:T(8,128)(2,1)}), bf16[3,4096,1024]{2,1,0:T(8,128)(2,1)}) %all-gather.2.cloned.1.call-update) | async-done | bytes 25165840 | tf_op jit(solution)/shard_map/all_gather | solution.py:23
  301.0 3.0 broadcast_in_dim.23
  303.9 43.6 %while.10 = (s32[]{:T(128)}, f32[20,256,256]{2,1,0:T(8,128)}, s32[]{:T(128)}, s32[20]{0:T(128)S(1)}, bf16[3,4096,1024]{2,1,0:T(8,128)(2,1)}, /*index=5*/s32[20]{...) while((s32[]{:T(128)}, f32[20,256,256]{2,1,0:T(8,128)}, ...), condition=%wide.region_2.3_spmd, body=%wide.region_1.2_spmd.sunk | while | flops 402653184 | bytes 3408175 | solution.py:35
  304.6 0.6 dynamic_slice.31
  305.7 0.6 dynamic_slice.30
  306.9 3.2 fusion.19
  310.8 0.6 dynamic_slice.31
  311.9 0.6 dynamic_slice.30
  313.0 3.2 fusion.19
  316.9 0.6 dynamic_slice.31
  318.0 0.6 dynamic_slice.30
  319.1 3.2 fusion.19
  323.1 0.6 dynamic_slice.31
  324.2 0.6 dynamic_slice.30
  325.3 3.2 fusion.19
  329.2 0.6 dynamic_slice.31
  330.3 0.6 dynamic_slice.30
  331.4 3.2 fusion.19
  335.3 0.6 dynamic_slice.31
  336.4 0.6 dynamic_slice.30
  337.5 3.2 fusion.19
  341.4 0.6 dynamic_slice.31
  342.5 0.6 dynamic_slice.30
  343.7 3.2 fusion.19
  347.6 0.0 reduce-scatter.2.cloned.1.call-update
  347.6 0.6 copy-done
  348.2 152.2 %reduce-scatter.2.cloned.1.call-done = f32[20,16,256]{2,1,0:T(8,128)} async-done(((f32[20,256,256]{2,1,0:T(8,128)}), f32[20,16,256]{2,1,0:T(8,128)}) %reduce-scatter.2.cloned.1.call-update) | async-done | bytes 327696 | tf_op jit(solution)/shard_map/reduce_scatter | solution.py:36
  500.5 1.8 select_bitcast_fusion
  (3 shorter events, 0.0 us)
Async XLA Ops:
  6.5 294.4 %all-gather.2.cloned.1.call-start = ((), (), s32[]{:S(2)}) async-start(), calls=%async_computation.1 | async-start | bytes 26738688 | tf_op jit(solution)/shard_map/all_gather | solution.py:23
  7.3 493.2 %reduce-scatter.2.cloned.1.call-start = ((), (), s32[]{:S(2)}) async-start(), calls=%async_computation.2 | async-start | bytes 5570560 | tf_op jit(solution)/shard_map/reduce_scatter | solution.py:36
  347.6 0.7 copy-start
Sparse Core Ops, SparseCore 0:
  9.8 291.1 all-gather.1
  347.7 152.7 reduce-scatter.1
where the time goes:
time: 510 us; the launch traced here: 509 us
  waiting for transfers between devices  444 us (87%)
  matrix products  22.5 us (4%)
  between operations  13.4 us (3%)
  loops' own time  13.3 us (3%)
  local copies, waits for them, and re-layouts  12.1 us (2%)
    all_gather x1, waiting for transfers between devices, per_device(): whole = lax.all_gather(snapshots, 'tm', axis=1, tiled=True)  292 us
    reduce_scatter x1, waiting for transfers between devices, per_device(): lax.psum_scatter(partial_tiles, 'space', scatter_dimension=1, tiled=True)  152 us
    dot_general x7, matrix products, pair_tile(): jnp.einsum('kic,kjc->ij', left_block, right_block, preferred_element_type...  22.5 us
    another operation x1, loops' own time, per_device(): partial_tiles = lax.fori_loop(0, filled, add_tile, empty)  13.3 us
  transfers between devices with their start and end apart: 2, of which 2 were waited for; matrix products, arithmetic and copies ran while one was open for 0% of the time, Pallas kernels for 0%

commit v1 on v0

v1 whole, which is shorter than its diff:
```python
import math

import jax
import jax.numpy as jnp
from jax import lax
from jax.experimental import pallas as pl
from jax.experimental.pallas import tpu as pltpu
from jax.sharding import PartitionSpec as P

MESH = pl.DeviceIdType.MESH
BLOCK = 256
SIDE = 4
TILES = 34
BATCHES = (8, 9, 9, 8)


def pick(index, values):
    chosen = values[0]
    for place in range(1, len(values)):
        chosen = jnp.where(index == place, values[place], chosen)
    return chosen


def tile_list(h, y):
    z = [lax.rem(h + step, SIDE) for step in range(SIDE)]
    same, near, far = y, lax.rem(y + 1, SIDE), lax.rem(y + 2, SIDE)

    def make(z1, y1, z2, y2, tile):
        first = z1 * SIDE + y1 <= z2 * SIDE + y2
        one, two = y1 * SIDE + z1, y2 * SIDE + z2
        return (jnp.where(first, one, two), jnp.where(first, two, one), tile)

    def own(a, b):
        step = (b - a) % SIDE
        base = lax.rem(z[a], 2) if step == 2 else z[a]
        return make(z[a], same, z[b], same, 16 + 4 * step + base)

    def side(a, b):
        return make(z[a], same, z[b], near, SIDE * z[a] + z[b])

    def across(a):
        b = (a + 1) % SIDE
        return make(z[a], same, z[b], far, 26 + z[a])

    half = jnp.where(y >= 2, 2, 0)
    return [
        own(0, 0), side(0, 0),
        own(3, 3), own(3, 0), side(0, 3), side(3, 0), side(3, 3), across(3),
        own(1, 1), own(0, 1), own(1, 3), side(1, 1), side(1, 0), side(0, 1), side(1, 3), side(3, 1), across(0),
        own(2, 2), own(1, 2), own(2, 3), own(0, 2), side(2, 0), side(0, 2), side(2, 1), side(1, 2), side(2, 2),
        side(2, 3), side(3, 2), across(1), across(2),
        make(half, same, half, far, 30), make(half + 1, same, half + 1, far, 31),
        make(0, same, 2, far, 32), make(1, same, 3, far, 33),
    ]


def kernel(
    scale, x_ref, out_ref, blocks, relay, part, pair, xfirst, xlast, total, zhalf, zpart,
    local_sem, zs, zr, ys, yr, ps, pr, xs, xr, ws, wr,
):
    tm, space = lax.axis_index("tm"), lax.axis_index("space")
    h, y = tm // SIDE, lax.rem(tm, SIDE)
    x, low, core = space // SIDE, lax.rem(space // 2, 2), lax.rem(space, 2)

    def device(h_=h, y_=y, x_=x, low_=low, core_=core):
        return (h_ * SIDE + y_, x_ * SIDE + low_ * 2 + core_)

    def up(value, step, size=SIDE):
        return lax.rem(value + step, size)

    hp, hm, h2 = up(h, 1), up(h, 3), up(h, 2)
    yp, ym = up(y, 1), up(y, 3)
    xp, xm, x2 = up(x, 1), up(x, 3), up(x, 2)
    other = 1 - core
    place = h * 2 + low
    zp, zm = up(place, 1, 8), up(place, 7, 8)
    dev_hp, dev_hm = device(h_=hp), device(h_=hm)
    dev_yp, dev_ym = device(y_=yp), device(y_=ym)
    dev_xp, dev_xm = device(x_=xp), device(x_=xm)
    dev_zp = device(h_=zp // 2, low_=lax.rem(zp, 2))
    dev_zm = device(h_=zm // 2, low_=lax.rem(zm, 2))
    dev_pair = device(core_=other)

    barrier = pltpu.get_barrier_semaphore()
    peers = (dev_hp, dev_hm, dev_yp, dev_ym, dev_xp, dev_xm, dev_zp, dev_zm, dev_pair)
    for peer in peers:
        pl.semaphore_signal(barrier, inc=1, device_id=peer, device_id_type=MESH)
    pl.semaphore_wait(barrier, len(peers))

    started = []

    def send(src, dst, send_sem, recv_sem, peer):
        copy = pltpu.make_async_remote_copy(
            src_ref=src, dst_ref=dst, send_sem=send_sem, recv_sem=recv_sem, device_id=peer, device_id_type=MESH
        )
        copy.start()
        started.append(copy)
        return copy

    def cells(which):
        return pl.ds(pl.multiple_of(which * BLOCK, BLOCK), BLOCK)

    every = slice(None)
    first_rows, last_rows = pl.ds(0, BLOCK // 2), pl.ds(BLOCK // 2, BLOCK // 2)

    local = pltpu.make_async_copy(x_ref.at[:, :, cells(h)], blocks.at[y, h], local_sem)
    local.start()
    to_hp = send(x_ref.at[:, :, cells(hp)], blocks.at[y, h], zs.at[0], zr.at[0], dev_hp)
    to_hm = send(x_ref.at[:, :, cells(hm)], blocks.at[y, h], zs.at[1], zr.at[1], dev_hm)
    via_hp = send(x_ref.at[:, first_rows, cells(h2)], relay.at[0], zs.at[2], zr.at[2], dev_hp)
    via_hm = send(x_ref.at[:, last_rows, cells(h2)], relay.at[1], zs.at[3], zr.at[3], dev_hm)

    direct, onward = {}, {}

    def spread(key, z):
        down = send(blocks.at[y, z], blocks.at[y, z], ys.at[key, 0], yr.at[key, 0], dev_ym)
        above = send(blocks.at[y, z, pl.ds(1, 2)], blocks.at[y, z, pl.ds(1, 2)], ys.at[key, 1], yr.at[key, 1], dev_yp)
        direct[key] = (down, above)

    def forward(key, z):
        down, above = direct[key]
        down.wait_recv()
        first = send(blocks.at[yp, z, pl.ds(0, 1)], blocks.at[yp, z, pl.ds(0, 1)], ys.at[key, 2], yr.at[key, 2], dev_ym)
        above.wait_recv()
        rest = send(blocks.at[ym, z, pl.ds(1, 2)], blocks.at[ym, z, pl.ds(1, 2)], ys.at[key, 3], yr.at[key, 3], dev_yp)
        onward[key] = (first, rest)

    def gathered(key):
        for copy in onward[key]:
            copy.wait_recv()

    tiles = tile_list(h, y)
    starts = [sum(BATCHES[:number]) for number in range(len(BATCHES))]

    def compute(number):
        begin, size = starts[number], BATCHES[number]
        some = tiles[begin:begin + size]

        @pl.loop(0, size)
        def _(step):
            left = pick(step, [tile[0] for tile in some])
            right = pick(step, [tile[1] for tile in some])
            ly, lz, ry, rz = left // SIDE, lax.rem(left, SIDE), right // SIDE, lax.rem(right, SIDE)
            product = None
            for comp in range(3):
                term = lax.dot_general(
                    blocks[ly, lz, comp], blocks[ry, rz, comp], (((1,), (1,)), ((), ())),
                    preferred_element_type=jnp.float32,
                )
                product = term if product is None else product + term
            slot = begin + step
            for row in range(BLOCK // 8):
                for lane in range(2):
                    place_x, place_low, place_core, place_row = row // 8, row // 4 % 2, row // 2 % 2, row % 2
                    part[slot, place_core, place_x, place_low * 4 + place_row * 2 + lane] = product[
                        row * 8:row * 8 + 8, lane * 128:lane * 128 + 128
                    ]

        span = pl.ds(begin, size)
        return send(part.at[span, other], pair.at[span], ps.at[number], pr.at[number], dev_pair)

    def add_pair(number, copy):
        begin, size = starts[number], BATCHES[number]
        copy.wait_recv()

        @pl.loop(begin, begin + size)
        def _(slot):
            part[slot, core] = part[slot, core] + pair[slot]

        span = pl.ds(begin, size)
        return (
            send(part.at[span, core, x2, pl.ds(0, 4)], xfirst.at[0, span], xs.at[number, 0], xr.at[number, 0], dev_xp),
            send(part.at[span, core, x2, pl.ds(4, 4)], xfirst.at[1, span], xs.at[number, 1], xr.at[number, 1], dev_xm),
        )

    def add_first(number, copies):
        begin, size = starts[number], BATCHES[number]
        for copy in copies:
            copy.wait_recv()

        @pl.loop(begin, begin + size)
        def _(slot):
            part[slot, core, xp, 0:4] = part[slot, core, xp, 0:4] + xfirst[0, slot]
            part[slot, core, xm, 4:8] = part[slot, core, xm, 4:8] + xfirst[1, slot]

        span = pl.ds(begin, size)
        return (
            send(part.at[span, core, xp], xlast.at[0, span], xs.at[number, 2], xr.at[number, 2], dev_xp),
            send(part.at[span, core, xm], xlast.at[1, span], xs.at[number, 3], xr.at[number, 3], dev_xm),
        )

    def add_last(number, copies):
        begin, size = starts[number], BATCHES[number]
        for copy in copies:
            copy.wait_recv()
        some = tiles[begin:begin + size]

        @pl.loop(0, size)
        def _(step):
            slot = begin + step
            total[pick(step, [tile[2] for tile in some])] = part[slot, core, x] + xlast[0, slot] + xlast[1, slot]

    local.wait()
    spread(0, h)
    forward(0, h)
    to_hp.wait_recv()
    spread(1, hm)
    to_hm.wait_recv()
    spread(2, hp)
    via_hp.wait_recv()
    on_hp = send(relay.at[0], blocks.at[y, hm, :, first_rows], zs.at[4], zr.at[4], dev_hp)
    via_hm.wait_recv()
    on_hm = send(relay.at[1], blocks.at[y, hp, :, last_rows], zs.at[5], zr.at[5], dev_hm)
    gathered(0)
    forward(1, hm)
    forward(2, hp)
    on_hp.wait_recv()
    on_hm.wait_recv()
    spread(3, h2)
    gathered(1)
    pair0 = compute(0)
    gathered(2)
    pair1 = compute(1)
    first0 = add_pair(0, pair0)
    forward(3, h2)
    first1 = add_pair(1, pair1)
    last0 = add_first(0, first0)
    last1 = add_first(1, first1)
    gathered(3)
    pair2 = compute(2)
    pair3 = compute(3)
    first2 = add_pair(2, pair2)
    add_last(0, last0)
    first3 = add_pair(3, pair3)
    last2 = add_first(2, first2)
    add_last(1, last1)
    last3 = add_first(3, first3)
    add_last(2, last2)
    add_last(3, last3)

    def piece(step):
        target = up(place, step, 8)
        return lax.rem(target, 2) * 4 + target // 2

    four = piece(4)
    near_half, far_half = pl.ds(0, TILES // 2), pl.ds(TILES // 2, TILES // 2)
    go_up = send(total.at[near_half, four], zhalf.at[0], ws.at[0, 0], wr.at[0, 0], dev_zp)
    go_down = send(total.at[far_half, four], zhalf.at[1], ws.at[1, 0], wr.at[1, 0], dev_zm)
    for step in range(3):
        above, below = piece(3 - step), piece(5 + step)
        go_up.wait_recv()
        if step == 0:
            total[0:TILES // 2, above] = total[0:TILES // 2, above] + zhalf[0]
        else:
            total[:, above] = total[:, above] + zpart[0, step - 1]
        go_up = send(total.at[:, above], zpart.at[0, step], ws.at[0, step + 1], wr.at[0, step + 1], dev_zp)
        go_down.wait_recv()
        if step == 0:
            total[TILES // 2:TILES, below] = total[TILES // 2:TILES, below] + zhalf[1]
        else:
            total[:, below] = total[:, below] + zpart[1, step - 1]
        go_down = send(total.at[:, below], zpart.at[1, step], ws.at[1, step + 1], wr.at[1, step + 1], dev_zm)
    go_up.wait_recv()
    go_down.wait_recv()
    out_ref[...] = (total[:, piece(0)] + zpart[0, 2] + zpart[1, 2]) * scale
    for copy in started:
        copy.wait_send()


def reduced(snapshots, scale):
    count = len(BATCHES)
    dma = pltpu.SemaphoreType.DMA
    f32, b16 = jnp.float32, jnp.bfloat16
    return pl.pallas_call(
        lambda *refs: kernel(scale, *refs),
        out_shape=jax.ShapeDtypeStruct((TILES, 8, 128), f32),
        in_specs=[pl.BlockSpec(memory_space=pl.ANY)],
        out_specs=pl.BlockSpec(memory_space=pltpu.VMEM),
        scratch_shapes=[
            pltpu.VMEM((4, 4, 3, BLOCK, BLOCK), b16),
            pltpu.VMEM((2, 3, BLOCK // 2, BLOCK), b16),
            pltpu.VMEM((TILES, 2, 4, 8, 8, 128), f32),
            pltpu.VMEM((TILES, 4, 8, 8, 128), f32),
            pltpu.VMEM((2, TILES, 4, 8, 128), f32),
            pltpu.VMEM((2, TILES, 8, 8, 128), f32),
            pltpu.VMEM((TILES, 8, 8, 128), f32),
            pltpu.VMEM((2, TILES // 2, 8, 128), f32),
            pltpu.VMEM((2, 3, TILES, 8, 128), f32),
            dma(()), dma((6,)), dma((6,)), dma((4, 4)), dma((4, 4)), dma((count,)), dma((count,)),
            dma((count, 4)), dma((count, 4)), dma((2, 4)), dma((2, 4)),
        ],
        compiler_params=pltpu.CompilerParams(collective_id=0, has_side_effects=True, vmem_limit_bytes=60 * 2**20),
        name="gram_reduce",
    )(snapshots)


def tile_index(table):
    a, b = table[:, 0], table[:, 1]
    za, ya, zb, yb = a // SIDE, a % SIDE, b // SIDE, b % SIDE
    dy, dz = (yb - ya) % SIDE, (zb - za) % SIDE
    own = jnp.where(dz == 2, 24 + za % 2, jnp.where(dz == 3, 20 + zb, 16 + 4 * dz + za))
    low = za < 2
    far_y = jnp.where(dz == 3, yb, jnp.where((dz == 0) & ~low, yb, ya))
    far_t = jnp.where(
        dz == 1, 26 + za, jnp.where(dz == 3, 26 + zb, jnp.where(dz == 0, 30 + za % 2, 32 + za))
    )
    which_y = jnp.where(dy == 2, far_y, jnp.where(dy == 3, yb, ya))
    which_t = jnp.where(
        dy == 0, own, jnp.where(dy == 1, 4 * za + zb, jnp.where(dy == 3, 4 * zb + za, far_t))
    )
    return jnp.where(a >= 0, which_y * TILES + which_t, SIDE * TILES)


def per_device(snapshots, tile_table):
    cells_dev = snapshots.shape[2]
    scale = 1.0 / math.sqrt(3 * cells_dev * lax.axis_size("space"))
    table = tile_table[0]
    index = tile_index(table)
    pieces = reduced(snapshots, scale)
    whole = lax.all_gather(pieces, "tm", axis=0, tiled=False)
    whole = whole.reshape(SIDE, SIDE * TILES, 8, 128)
    chosen = jnp.take(whole, jnp.minimum(index, SIDE * TILES - 1), axis=1)
    chosen = jnp.where((index < SIDE * TILES)[None, :, None, None], chosen, jnp.zeros_like(chosen))
    slots = table.shape[0]
    chosen = chosen.reshape(2, 2, slots, 8, 128).transpose(2, 0, 3, 1, 4)
    return chosen.reshape(1, slots, 16, BLOCK)


def solution(mesh):
    in_specs = (P(None, "tm", "space"), P("tm", None, None))
    out_specs = P("tm", None, "space", None)
    return jax.shard_map(
        per_device, mesh=mesh, in_specs=in_specs, out_specs=out_specs, check_vma=False
    )
```

time: 510 us -> 193 us (0.38)
  waiting for transfers between devices: 444 us -> 57.9 us
  Pallas kernels: 0 us -> 117 us
  matrix products: 22.5 us -> 0 us
  loops' own time: 13.3 us -> 0 us
  local copies, waits for them, and re-layouts: 12.1 us -> 2.21 us
    all_gather x1, waiting for transfers between devices: 292 us -> 57.8 us  [per_device(): whole = lax.all_gather(pieces, 'tm', axis=0, tiled=False)]
    reduce_scatter x1 -> x0, waiting for transfers between devices: 152 us -> none  [per_device(): lax.psum_scatter(partial_tiles, 'space', scatter_dimension=1, tiled=True)]
    pallas_call x0 -> x1, Pallas kernels: none -> 117 us  [reduced(): pl.pallas_call(lambda *refs: kernel(scale, *refs), out_shape=jax.ShapeDty...]
    dot_general x7 -> x0, matrix products: 22.5 us -> none  [pair_tile(): jnp.einsum('kic,kjc->ij', left_block, right_block, preferred_element_type...]
    another operation x1 -> x0, loops' own time: 13.3 us -> none  [per_device(): partial_tiles = lax.fori_loop(0, filled, add_tile, empty)]
    dynamic_slice x14 -> x0, local copies, waits for them, and re-layouts: 7.76 us -> none  [the longest x7 3.89 us: add_tile(): second = jnp.maximum(col_block[slot], 0)]
  transfers between devices with their start and end apart: 2 -> 1, of which waited for: 2 -> 1; matrix products, arithmetic and copies ran while one was open for 0% -> 1% of each run, Pallas kernels for 0% -> 0%
where the time goes in v1:
time: 193 us; the launch traced here: 192 us
  Pallas kernels  117 us (61%)
  waiting for transfers between devices  57.9 us (30%)
  between operations  13.4 us (7%)
  other arithmetic  2.42 us (1%)
  local copies, waits for them, and re-layouts  2.21 us (1%)
    pallas_call x1, Pallas kernels, reduced(): pl.pallas_call(lambda *refs: kernel(scale, *refs), out_shape=jax.ShapeDty...  117 us
    all_gather x1, waiting for transfers between devices, per_device(): whole = lax.all_gather(pieces, 'tm', axis=0, tiled=False)  57.8 us
  transfers between devices with their start and end apart: 1, of which 1 were waited for; matrix products, arithmetic and copies ran while one was open for 1% of the time, Pallas kernels for 0%

profile of v1, /device:TPU:16, one launch (start us, length us, event | category | flops | bytes accessed | tf_op | source)
XLA Modules:
  0.0 192.5 jit_solution(17503333357583009639)
XLA Ops:
  6.5 0.0 all-gather.3.cloned.1.call-start
  6.5 116.6 %gram_reduce.1 = f32[34,8,128]{2,1,0:T(8,128)} custom-call(bf16[3,256,1024]{2,1,0:T(8,128)(2,1)} %refs_0_.1), custom_call_target="tpu_custom_call" | custom-call | tf_op jit(solution)/shard_map/gram_reduce/pallas_call | solution.py:274
  123.1 0.0 all-gather.3.cloned.1.call-update
  123.1 0.8 and_bitcast_fusion
  123.9 0.8 fusion.4
  124.7 57.8 %all-gather.3.cloned.1.call-done = f32[544,8,128]{2,1,0:T(8,128)} async-done(((f32[34,8,128]{2,1,0:T(8,128)}), f32[544,8,128]{2,1,0:T(8,128)}) %all-gather.3.cloned.1.call-update) | async-done | bytes 2228240 | tf_op jit(solution)/shard_map/all_gather | solution.py:320
  182.6 2.2 %gather_fusion = f32[20,4,8,128]{3,2,1,0:T(8,128)S(1)} fusion(f32[4,136,8,128]{3,2,1,0:T(8,128)} %bitcast.40, s32[1024]{0:T(1024)S(1)} %pad_clamp_fusion), kind=kCustom, calls=%fused_computation | custom fusion | bytes 655440 | tf_op jit(solution)/shard_map/jit(_take)/gather | solution.py:322
  184.8 0.8 select_bitcast_fusion
  (1 shorter events, 0.0 us)
Async XLA Ops:
  6.5 176.0 %all-gather.3.cloned.1.call-start = ((), (), s32[]{:S(2)}) async-start(), calls=%async_computation | async-start | bytes 2367488 | tf_op jit(solution)/shard_map/all_gather | solution.py:320
Sparse Core Ops, SparseCore 0:
  123.3 59.2 all-gather.2

commit v2 on v1

--- a/solution.py
+++ b/solution.py
@@ -10,6 +10,7 @@
 MESH = pl.DeviceIdType.MESH
 BLOCK = 256
 SIDE = 4
+SLOTS = 20
 TILES = 34
 BATCHES = (8, 9, 9, 8)
 
@@ -55,8 +56,9 @@
 
 
 def kernel(
-    scale, x_ref, out_ref, blocks, relay, part, pair, xfirst, xlast, total, zhalf, zpart,
-    local_sem, zs, zr, ys, yr, ps, pr, xs, xr, ws, wr,
+    scale, x_ref, index_ref, out_ref, blocks, relay, part, pair, xfirst, xlast, total, zhalf, zpart,
+    indices, wanted, pieces, chosen, through, landed,
+    local_sem, zs, zr, ys, yr, ps, pr, xs, xr, ws, wr, ts, tr, gs, gr, os, onr,
 ):
     tm, space = lax.axis_index("tm"), lax.axis_index("space")
     h, y = tm // SIDE, lax.rem(tm, SIDE)
@@ -74,7 +76,7 @@
     other = 1 - core
     place = h * 2 + low
     zp, zm = up(place, 1, 8), up(place, 7, 8)
-    dev_hp, dev_hm = device(h_=hp), device(h_=hm)
+    dev_hp, dev_hm, dev_h2 = device(h_=hp), device(h_=hm), device(h_=h2)
     dev_yp, dev_ym = device(y_=yp), device(y_=ym)
     dev_xp, dev_xm = device(x_=xp), device(x_=xm)
     dev_zp = device(h_=zp // 2, low_=lax.rem(zp, 2))
@@ -82,7 +84,7 @@
     dev_pair = device(core_=other)
 
     barrier = pltpu.get_barrier_semaphore()
-    peers = (dev_hp, dev_hm, dev_yp, dev_ym, dev_xp, dev_xm, dev_zp, dev_zm, dev_pair)
+    peers = (dev_hp, dev_hm, dev_h2, dev_yp, dev_ym, dev_xp, dev_xm, dev_zp, dev_zm, dev_pair)
     for peer in peers:
         pl.semaphore_signal(barrier, inc=1, device_id=peer, device_id_type=MESH)
     pl.semaphore_wait(barrier, len(peers))
@@ -105,10 +107,17 @@
 
     local = pltpu.make_async_copy(x_ref.at[:, :, cells(h)], blocks.at[y, h], local_sem)
     local.start()
+    own_index = pltpu.make_async_copy(index_ref, indices.at[h], ts.at[3])
+    own_index.start()
     to_hp = send(x_ref.at[:, :, cells(hp)], blocks.at[y, h], zs.at[0], zr.at[0], dev_hp)
     to_hm = send(x_ref.at[:, :, cells(hm)], blocks.at[y, h], zs.at[1], zr.at[1], dev_hm)
     via_hp = send(x_ref.at[:, first_rows, cells(h2)], relay.at[0], zs.at[2], zr.at[2], dev_hp)
     via_hm = send(x_ref.at[:, last_rows, cells(h2)], relay.at[1], zs.at[3], zr.at[3], dev_hm)
+
+    told = [
+        send(index_ref, indices.at[h], ts.at[number], tr.at[number], peer)
+        for number, peer in enumerate((dev_hp, dev_hm, dev_h2))
+    ]
 
     direct, onward = {}, {}
 
@@ -262,19 +271,68 @@
         go_down = send(total.at[:, below], zpart.at[1, step], ws.at[1, step + 1], wr.at[1, step + 1], dev_zm)
     go_up.wait_recv()
     go_down.wait_recv()
-    out_ref[...] = (total[:, piece(0)] + zpart[0, 2] + zpart[1, 2]) * scale
+    mine = pl.ds(y * TILES, TILES)
+    pieces[mine] = (total[:, piece(0)] + zpart[0, 2] + zpart[1, 2]) * scale
+    pieces[SIDE * TILES] = jnp.zeros((8, 128), jnp.float32)
+
+    to_yp = send(pieces.at[mine], pieces.at[mine], gs.at[0], gr.at[0], dev_yp)
+    to_ym = send(pieces.at[mine], pieces.at[mine], gs.at[1], gr.at[1], dev_ym)
+    own_index.wait()
+    for copy in told:
+        copy.wait_recv()
+    listed = pltpu.make_async_copy(indices, wanted, local_sem)
+    listed.start()
+    listed.wait()
+    to_yp.wait_recv()
+    early = pl.ds(ym * TILES, TILES // 2)
+    on_yp = send(pieces.at[early], pieces.at[early], gs.at[2], gr.at[2], dev_yp)
+    to_ym.wait_recv()
+    late = pl.ds(yp * TILES + TILES // 2, TILES // 2)
+    on_ym = send(pieces.at[late], pieces.at[late], gs.at[3], gr.at[3], dev_ym)
+    on_yp.wait_recv()
+    on_ym.wait_recv()
+
+    def choose(number, z):
+        @pl.loop(0, SLOTS)
+        def _(slot):
+            chosen[number, slot] = pieces[wanted[z, 0, slot]]
+
+    half = SLOTS // 2
+    choose(2, h2)
+    far_hp = send(chosen.at[2, pl.ds(0, half)], through.at[0], os.at[2], onr.at[2], dev_hp)
+    far_hm = send(chosen.at[2, pl.ds(half, half)], through.at[1], os.at[3], onr.at[3], dev_hm)
+    choose(0, hp)
+    out_hp = send(chosen.at[0], landed.at[0], os.at[0], onr.at[0], dev_hp)
+    choose(1, hm)
+    out_hm = send(chosen.at[1], landed.at[1], os.at[1], onr.at[1], dev_hm)
+    far_hp.wait_recv()
+    last_hp = send(through.at[0], landed.at[2, pl.ds(0, half)], os.at[4], onr.at[4], dev_hp)
+    far_hm.wait_recv()
+    last_hm = send(through.at[1], landed.at[2, pl.ds(half, half)], os.at[5], onr.at[5], dev_hm)
+
+    @pl.loop(0, SLOTS)
+    def _(slot):
+        out_ref[h, slot] = pieces[wanted[h, 0, slot]]
+
+    out_hp.wait_recv()
+    out_ref[hm] = landed[0]
+    out_hm.wait_recv()
+    out_ref[hp] = landed[1]
+    last_hp.wait_recv()
+    last_hm.wait_recv()
+    out_ref[h2] = landed[2]
     for copy in started:
         copy.wait_send()
 
 
-def reduced(snapshots, scale):
+def gram(snapshots, index, scale):
     count = len(BATCHES)
     dma = pltpu.SemaphoreType.DMA
     f32, b16 = jnp.float32, jnp.bfloat16
     return pl.pallas_call(
         lambda *refs: kernel(scale, *refs),
-        out_shape=jax.ShapeDtypeStruct((TILES, 8, 128), f32),
-        in_specs=[pl.BlockSpec(memory_space=pl.ANY)],
+        out_shape=jax.ShapeDtypeStruct((SIDE, SLOTS, 8, 128), f32),
+        in_specs=[pl.BlockSpec(memory_space=pl.ANY)] * 2,
         out_specs=pl.BlockSpec(memory_space=pltpu.VMEM),
         scratch_shapes=[
             pltpu.VMEM((4, 4, 3, BLOCK, BLOCK), b16),
@@ -286,12 +344,19 @@
             pltpu.VMEM((TILES, 8, 8, 128), f32),
             pltpu.VMEM((2, TILES // 2, 8, 128), f32),
             pltpu.VMEM((2, 3, TILES, 8, 128), f32),
+            pltpu.VMEM((SIDE, 8, 128), jnp.int32),
+            pltpu.SMEM((SIDE, 8, 128), jnp.int32),
+            pltpu.VMEM((SIDE * TILES + 1, 8, 128), f32),
+            pltpu.VMEM((3, SLOTS, 8, 128), f32),
+            pltpu.VMEM((2, SLOTS // 2, 8, 128), f32),
+            pltpu.VMEM((3, SLOTS, 8, 128), f32),
             dma(()), dma((6,)), dma((6,)), dma((4, 4)), dma((4, 4)), dma((count,)), dma((count,)),
             dma((count, 4)), dma((count, 4)), dma((2, 4)), dma((2, 4)),
+            dma((4,)), dma((3,)), dma((4,)), dma((4,)), dma((6,)), dma((6,)),
         ],
         compiler_params=pltpu.CompilerParams(collective_id=0, has_side_effects=True, vmem_limit_bytes=60 * 2**20),
-        name="gram_reduce",
-    )(snapshots)
+        name="gram_tiles",
+    )(snapshots, index)
 
 
 def tile_index(table):
@@ -315,15 +380,10 @@
     cells_dev = snapshots.shape[2]
     scale = 1.0 / math.sqrt(3 * cells_dev * lax.axis_size("space"))
     table = tile_table[0]
-    index = tile_index(table)
-    pieces = reduced(snapshots, scale)
-    whole = lax.all_gather(pieces, "tm", axis=0, tiled=False)
-    whole = whole.reshape(SIDE, SIDE * TILES, 8, 128)
-    chosen = jnp.take(whole, jnp.minimum(index, SIDE * TILES - 1), axis=1)
-    chosen = jnp.where((index < SIDE * TILES)[None, :, None, None], chosen, jnp.zeros_like(chosen))
     slots = table.shape[0]
-    chosen = chosen.reshape(2, 2, slots, 8, 128).transpose(2, 0, 3, 1, 4)
-    return chosen.reshape(1, slots, 16, BLOCK)
+    index = jnp.broadcast_to(jnp.pad(tile_index(table), (0, 128 - slots)), (8, 128))
+    tiles = gram(snapshots, index, scale).reshape(2, 2, slots, 8, 128)
+    return tiles.transpose(2, 0, 3, 1, 4).reshape(1, slots, 16, BLOCK)
 
 
 def solution(mesh):

time: 193 us -> 140 us (0.73)
  waiting for transfers between devices: 57.9 us -> 0 us
  Pallas kernels: 117 us -> 135 us
  between operations: 13.4 us -> 0.02 us
    all_gather x1 -> x0, waiting for transfers between devices: 57.8 us -> none  [per_device(): whole = lax.all_gather(pieces, 'tm', axis=0, tiled=False)]
    pallas_call x1, Pallas kernels: 117 us -> 135 us  [gram(): pl.pallas_call(lambda *refs: kernel(scale, *refs), out_shape=jax.ShapeDty...]
    gather x1 -> x0, local copies, waits for them, and re-layouts: 2.21 us -> none  [per_device(): chosen = jnp.take(whole, jnp.minimum(index, SIDE * TILES - 1), axis=1)]
  transfers between devices with their start and end apart: 1 -> 0, of which waited for: 1 -> 0; matrix products, arithmetic and copies ran while one was open for 1% -> 0% of each run, Pallas kernels for 0% -> 0%
where the time goes in v2:
time: 140 us; the launch traced here: 138 us
  Pallas kernels  135 us (96%)
  local copies, waits for them, and re-layouts  2.33 us (2%)
    pallas_call x1, Pallas kernels, gram(): pl.pallas_call(lambda *refs: kernel(scale, *refs), out_shape=jax.ShapeDty...  135 us

profile of v2, /device:TPU:16, one launch (start us, length us, event | category | flops | bytes accessed | tf_op | source)
XLA Modules:
  0.0 138.2 jit_solution(10026429064590071198)
XLA Ops:
  0.0 0.8 compare_select_fusion.11
  0.8 0.6 broadcast_in_dim.8.refs_1_
  1.4 135.1 %gram_tiles.1 = f32[4,20,8,128]{3,2,1,0:T(8,128)} custom-call(bf16[3,256,1024]{2,1,0:T(8,128)(2,1)} %refs_0_.1, s32[8,128]{1,0:T(8,128)} %broadcast_in_dim.8.refs_1_), custom_call_target="tpu_custom_call" | custom-call | tf_op jit(solution)/shard_map/gram_tiles/pallas_call | solution.py:332
  136.5 1.7 %copy.5 = f32[20,2,8,2,128]{4,2,3,1,0:T(8,128)} copy(f32[20,2,8,2,128]{4,2,0,3,1:T(8,128)} %bitcast.34) | data formatting | bytes 655360 | tf_op jit(solution)/shard_map/transpose | solution.py:386
  (1 shorter events, 0.0 us)

commit v3 on v2

--- a/solution.py
+++ b/solution.py
@@ -12,7 +12,8 @@
 SIDE = 4
 SLOTS = 20
 TILES = 34
-BATCHES = (8, 9, 9, 8)
+BATCHES = (8, 9, 6, 6, 5)
+CHUNKS = ((0, 16), (16, 18))
 
 
 def pick(index, values):
@@ -56,7 +57,7 @@
 
 
 def kernel(
-    scale, x_ref, index_ref, out_ref, blocks, relay, part, pair, xfirst, xlast, total, zhalf, zpart,
+    scale, x_ref, index_ref, out_ref, blocks, relay, part, pair, xfirst, xlast, total, zpart,
     indices, wanted, pieces, chosen, through, landed,
     local_sem, zs, zr, ys, yr, ps, pr, xs, xr, ws, wr, ts, tr, gs, gr, os, onr,
 ):
@@ -109,34 +110,54 @@
     local.start()
     own_index = pltpu.make_async_copy(index_ref, indices.at[h], ts.at[3])
     own_index.start()
-    to_hp = send(x_ref.at[:, :, cells(hp)], blocks.at[y, h], zs.at[0], zr.at[0], dev_hp)
-    to_hm = send(x_ref.at[:, :, cells(hm)], blocks.at[y, h], zs.at[1], zr.at[1], dev_hm)
-    via_hp = send(x_ref.at[:, first_rows, cells(h2)], relay.at[0], zs.at[2], zr.at[2], dev_hp)
-    via_hm = send(x_ref.at[:, last_rows, cells(h2)], relay.at[1], zs.at[3], zr.at[3], dev_hm)
-
+    comps = range(3)
+    to_hp = [send(x_ref.at[k, :, cells(hp)], blocks.at[y, h, k], zs.at[0, k], zr.at[0, k], dev_hp) for k in comps]
+    to_hm = [send(x_ref.at[k, :, cells(hm)], blocks.at[y, h, k], zs.at[1, k], zr.at[1, k], dev_hm) for k in comps]
+
+    moved, passed = {}, {}
+
+    def spread(key, z, k, src=None):
+        src = blocks.at[y, z, k] if src is None else src
+        dst = blocks.at[y, z, k]
+        moved[key, k, 0] = send(src, dst, ys.at[key, k, 0], yr.at[key, k, 0], dev_ym)
+        if k > 0:
+            moved[key, k, 1] = send(src, dst, ys.at[key, k, 1], yr.at[key, k, 1], dev_yp)
+
+    def forward(key, z, k):
+        if k == 0:
+            moved[key, k, 0].wait_recv()
+            block, peer = blocks.at[yp, z, k], dev_ym
+        else:
+            moved[key, k, 1].wait_recv()
+            block, peer = blocks.at[ym, z, k], dev_yp
+        passed[key, k] = send(block, block, ys.at[key, k, 2], yr.at[key, k, 2], peer)
+
+    def gathered(key):
+        for k in comps:
+            if k > 0:
+                moved[key, k, 0].wait_recv()
+            passed[key, k].wait_recv()
+
+    for k in comps:
+        spread(0, h, k, x_ref.at[k, :, cells(h)])
+    via_hp = [send(x_ref.at[k, first_rows, cells(h2)], relay.at[0, k], zs.at[2, k], zr.at[2, k], dev_hp) for k in comps]
+    via_hm = [send(x_ref.at[k, last_rows, cells(h2)], relay.at[1, k], zs.at[3, k], zr.at[3, k], dev_hm) for k in comps]
     told = [
         send(index_ref, indices.at[h], ts.at[number], tr.at[number], peer)
         for number, peer in enumerate((dev_hp, dev_hm, dev_h2))
     ]
-
-    direct, onward = {}, {}
-
-    def spread(key, z):
-        down = send(blocks.at[y, z], blocks.at[y, z], ys.at[key, 0], yr.at[key, 0], dev_ym)
-        above = send(blocks.at[y, z, pl.ds(1, 2)], blocks.at[y, z, pl.ds(1, 2)], ys.at[key, 1], yr.at[key, 1], dev_yp)
-        direct[key] = (down, above)
-
-    def forward(key, z):
-        down, above = direct[key]
-        down.wait_recv()
-        first = send(blocks.at[yp, z, pl.ds(0, 1)], blocks.at[yp, z, pl.ds(0, 1)], ys.at[key, 2], yr.at[key, 2], dev_ym)
-        above.wait_recv()
-        rest = send(blocks.at[ym, z, pl.ds(1, 2)], blocks.at[ym, z, pl.ds(1, 2)], ys.at[key, 3], yr.at[key, 3], dev_yp)
-        onward[key] = (first, rest)
-
-    def gathered(key):
-        for copy in onward[key]:
-            copy.wait_recv()
+    on_hp, on_hm = {}, {}
+
+    def onward(k):
+        via_hp[k].wait_recv()
+        on_hp[k] = send(relay.at[0, k], blocks.at[y, hm, k, first_rows], zs.at[4, k], zr.at[4, k], dev_hp)
+        via_hm[k].wait_recv()
+        on_hm[k] = send(relay.at[1, k], blocks.at[y, hp, k, last_rows], zs.at[5, k], zr.at[5, k], dev_hm)
+
+    def spread_far(k):
+        on_hp[k].wait_recv()
+        on_hm[k].wait_recv()
+        spread(3, h2, k)
 
     tiles = tile_list(h, y)
     starts = [sum(BATCHES[:number]) for number in range(len(BATCHES))]
@@ -209,88 +230,116 @@
             slot = begin + step
             total[pick(step, [tile[2] for tile in some])] = part[slot, core, x] + xlast[0, slot] + xlast[1, slot]
 
+    for k in comps:
+        forward(0, h, k)
+    for k in comps:
+        to_hp[k].wait_recv()
+        spread(1, hm, k)
+    to_hm[0].wait_recv()
+    spread(2, hp, 0)
+    forward(1, hm, 0)
+    forward(1, hm, 1)
+    to_hm[1].wait_recv()
+    spread(2, hp, 1)
+    onward(0)
+    forward(1, hm, 2)
+    to_hm[2].wait_recv()
+    spread(2, hp, 2)
+    onward(1)
+    onward(2)
+    forward(2, hp, 0)
+    forward(2, hp, 1)
     local.wait()
-    spread(0, h)
-    forward(0, h)
-    to_hp.wait_recv()
-    spread(1, hm)
-    to_hm.wait_recv()
-    spread(2, hp)
-    via_hp.wait_recv()
-    on_hp = send(relay.at[0], blocks.at[y, hm, :, first_rows], zs.at[4], zr.at[4], dev_hp)
-    via_hm.wait_recv()
-    on_hm = send(relay.at[1], blocks.at[y, hp, :, last_rows], zs.at[5], zr.at[5], dev_hm)
     gathered(0)
-    forward(1, hm)
-    forward(2, hp)
-    on_hp.wait_recv()
-    on_hm.wait_recv()
-    spread(3, h2)
     gathered(1)
     pair0 = compute(0)
+    forward(2, hp, 2)
+    spread_far(0)
+    first0 = add_pair(0, pair0)
+    spread_far(1)
+    last0 = add_first(0, first0)
+    spread_far(2)
     gathered(2)
     pair1 = compute(1)
-    first0 = add_pair(0, pair0)
-    forward(3, h2)
+    forward(3, h2, 0)
     first1 = add_pair(1, pair1)
-    last0 = add_first(0, first0)
+    forward(3, h2, 1)
     last1 = add_first(1, first1)
+    forward(3, h2, 2)
+    add_last(0, last0)
     gathered(3)
     pair2 = compute(2)
     pair3 = compute(3)
     first2 = add_pair(2, pair2)
-    add_last(0, last0)
+    pair4 = compute(4)
     first3 = add_pair(3, pair3)
+    add_last(1, last1)
+    first4 = add_pair(4, pair4)
     last2 = add_first(2, first2)
-    add_last(1, last1)
     last3 = add_first(3, first3)
+    last4 = add_first(4, first4)
     add_last(2, last2)
     add_last(3, last3)
+    add_last(4, last4)
 
     def piece(step):
         target = up(place, step, 8)
         return lax.rem(target, 2) * 4 + target // 2
 
-    four = piece(4)
-    near_half, far_half = pl.ds(0, TILES // 2), pl.ds(TILES // 2, TILES // 2)
-    go_up = send(total.at[near_half, four], zhalf.at[0], ws.at[0, 0], wr.at[0, 0], dev_zp)
-    go_down = send(total.at[far_half, four], zhalf.at[1], ws.at[1, 0], wr.at[1, 0], dev_zm)
-    for step in range(3):
-        above, below = piece(3 - step), piece(5 + step)
-        go_up.wait_recv()
-        if step == 0:
-            total[0:TILES // 2, above] = total[0:TILES // 2, above] + zhalf[0]
-        else:
-            total[:, above] = total[:, above] + zpart[0, step - 1]
-        go_up = send(total.at[:, above], zpart.at[0, step], ws.at[0, step + 1], wr.at[0, step + 1], dev_zp)
-        go_down.wait_recv()
-        if step == 0:
-            total[TILES // 2:TILES, below] = total[TILES // 2:TILES, below] + zhalf[1]
-        else:
-            total[:, below] = total[:, below] + zpart[1, step - 1]
-        go_down = send(total.at[:, below], zpart.at[1, step], ws.at[1, step + 1], wr.at[1, step + 1], dev_zm)
-    go_up.wait_recv()
-    go_down.wait_recv()
-    mine = pl.ds(y * TILES, TILES)
-    pieces[mine] = (total[:, piece(0)] + zpart[0, 2] + zpart[1, 2]) * scale
+    rings = ((0, 0, 4), (1, 1, 4), (0, 1, 3), (1, 0, 3))
+    flying = {}
+
+    def pass_on(chunk, way, hops, number):
+        begin, size = CHUNKS[chunk]
+        span = pl.ds(begin, size)
+        distance = hops - number
+        which = piece(distance if way == 0 else 8 - distance)
+        if number > 0:
+            flying[chunk, way].wait_recv()
+            total[begin:begin + size, which] = total[begin:begin + size, which] + zpart[way, number - 1, begin:begin + size]
+        flying[chunk, way] = send(
+            total.at[span, which], zpart.at[way, number, span],
+            ws.at[chunk, way, number], wr.at[chunk, way, number], dev_zp if way == 0 else dev_zm,
+        )
+
+    for number in range(4):
+        for chunk, way, hops in rings:
+            if number < hops:
+                pass_on(chunk, way, hops, number)
+
     pieces[SIDE * TILES] = jnp.zeros((8, 128), jnp.float32)
-
-    to_yp = send(pieces.at[mine], pieces.at[mine], gs.at[0], gr.at[0], dev_yp)
-    to_ym = send(pieces.at[mine], pieces.at[mine], gs.at[1], gr.at[1], dev_ym)
+    shared, onto = {}, {}
+    for chunk, (begin, size) in enumerate(CHUNKS):
+        for way in range(2):
+            flying[chunk, way].wait_recv()
+        up_last, down_last = (3, 2) if chunk == 0 else (2, 3)
+        end = begin + size
+        value = total[begin:end, piece(0)] + zpart[0, up_last, begin:end] + zpart[1, down_last, begin:end]
+        span = pl.ds(y * TILES + begin, size)
+        pieces[span] = value * scale
+        shared[chunk] = (
+            send(pieces.at[span], pieces.at[span], gs.at[chunk, 0], gr.at[chunk, 0], dev_yp),
+            send(pieces.at[span], pieces.at[span], gs.at[chunk, 1], gr.at[chunk, 1], dev_ym),
+        )
     own_index.wait()
     for copy in told:
         copy.wait_recv()
     listed = pltpu.make_async_copy(indices, wanted, local_sem)
     listed.start()
     listed.wait()
-    to_yp.wait_recv()
-    early = pl.ds(ym * TILES, TILES // 2)
-    on_yp = send(pieces.at[early], pieces.at[early], gs.at[2], gr.at[2], dev_yp)
-    to_ym.wait_recv()
-    late = pl.ds(yp * TILES + TILES // 2, TILES // 2)
-    on_ym = send(pieces.at[late], pieces.at[late], gs.at[3], gr.at[3], dev_ym)
-    on_yp.wait_recv()
-    on_ym.wait_recv()
+    for chunk, (begin, size) in enumerate(CHUNKS):
+        half = size // 2
+        to_yp, to_ym = shared[chunk]
+        to_yp.wait_recv()
+        early = pl.ds(ym * TILES + begin, half)
+        on_yp = send(pieces.at[early], pieces.at[early], gs.at[chunk, 2], gr.at[chunk, 2], dev_yp)
+        to_ym.wait_recv()
+        late = pl.ds(yp * TILES + begin + half, half)
+        on_ym = send(pieces.at[late], pieces.at[late], gs.at[chunk, 3], gr.at[chunk, 3], dev_ym)
+        onto[chunk] = (on_yp, on_ym)
+    for chunk in range(len(CHUNKS)):
+        for copy in onto[chunk]:
+            copy.wait_recv()
 
     def choose(number, z):
         @pl.loop(0, SLOTS)
@@ -342,17 +391,16 @@
             pltpu.VMEM((2, TILES, 4, 8, 128), f32),
             pltpu.VMEM((2, TILES, 8, 8, 128), f32),
             pltpu.VMEM((TILES, 8, 8, 128), f32),
-            pltpu.VMEM((2, TILES // 2, 8, 128), f32),
-            pltpu.VMEM((2, 3, TILES, 8, 128), f32),
+            pltpu.VMEM((2, 4, TILES, 8, 128), f32),
             pltpu.VMEM((SIDE, 8, 128), jnp.int32),
             pltpu.SMEM((SIDE, 8, 128), jnp.int32),
             pltpu.VMEM((SIDE * TILES + 1, 8, 128), f32),
             pltpu.VMEM((3, SLOTS, 8, 128), f32),
             pltpu.VMEM((2, SLOTS // 2, 8, 128), f32),
             pltpu.VMEM((3, SLOTS, 8, 128), f32),
-            dma(()), dma((6,)), dma((6,)), dma((4, 4)), dma((4, 4)), dma((count,)), dma((count,)),
-            dma((count, 4)), dma((count, 4)), dma((2, 4)), dma((2, 4)),
-            dma((4,)), dma((3,)), dma((4,)), dma((4,)), dma((6,)), dma((6,)),
+            dma(()), dma((6, 3)), dma((6, 3)), dma((4, 3, 3)), dma((4, 3, 3)), dma((count,)), dma((count,)),
+            dma((count, 4)), dma((count, 4)), dma((2, 2, 4)), dma((2, 2, 4)),
+            dma((4,)), dma((3,)), dma((2, 4)), dma((2, 4)), dma((6,)), dma((6,)),
         ],
         compiler_params=pltpu.CompilerParams(collective_id=0, has_side_effects=True, vmem_limit_bytes=60 * 2**20),
         name="gram_tiles",

time: 140 us -> 133 us (0.950); the launches traced: 138 us -> 133 us
  Pallas kernels: 135 us -> 130 us
    pallas_call x1, Pallas kernels: 135 us -> 130 us  [gram(): pl.pallas_call(lambda *refs: kernel(scale, *refs), out_shape=jax.ShapeDty...]
where the time goes in v3:
time: 133 us
  Pallas kernels  130 us (98%)
  local copies, waits for them, and re-layouts  2.33 us (2%)
    pallas_call x1, Pallas kernels, gram(): pl.pallas_call(lambda *refs: kernel(scale, *refs), out_shape=jax.ShapeDty...  130 us

profile of v3, /device:TPU:16, one launch (start us, length us, event | category | flops | bytes accessed | tf_op | source)
XLA Modules:
  0.0 132.6 jit_solution(16208669670140499149)
XLA Ops:
  0.0 0.8 compare_select_fusion.11
  0.8 0.6 broadcast_in_dim.8.refs_1_
  1.4 129.5 %gram_tiles.1 = f32[4,20,8,128]{3,2,1,0:T(8,128)} custom-call(bf16[3,256,1024]{2,1,0:T(8,128)(2,1)} %refs_0_.1, s32[8,128]{1,0:T(8,128)} %broadcast_in_dim.8.refs_1_), custom_call_target="tpu_custom_call" | custom-call | tf_op jit(solution)/shard_map/gram_tiles/pallas_call | solution.py:381
  130.9 1.7 %copy.5 = f32[20,2,8,2,128]{4,2,3,1,0:T(8,128)} copy(f32[20,2,8,2,128]{4,2,0,3,1:T(8,128)} %bitcast.34) | data formatting | bytes 655360 | tf_op jit(solution)/shard_map/transpose | solution.py:434
  (1 shorter events, 0.0 us)

commit v4 on v3

--- a/solution.py
+++ b/solution.py
@@ -25,7 +25,7 @@
 
 def tile_list(h, y):
     z = [lax.rem(h + step, SIDE) for step in range(SIDE)]
-    same, near, far = y, lax.rem(y + 1, SIDE), lax.rem(y + 2, SIDE)
+    same, near, back = y, lax.rem(y + 1, SIDE), lax.rem(y + 3, SIDE)
 
     def make(z1, y1, z2, y2, tile):
         first = z1 * SIDE + y1 <= z2 * SIDE + y2
@@ -42,17 +42,17 @@
 
     def across(a):
         b = (a + 1) % SIDE
-        return make(z[a], same, z[b], far, 26 + z[a])
-
-    half = jnp.where(y >= 2, 2, 0)
+        return make(z[a], back, z[b], near, 26 + z[a])
+
+    half = jnp.where(back >= 2, 2, 0)
     return [
         own(0, 0), side(0, 0),
         own(3, 3), own(3, 0), side(0, 3), side(3, 0), side(3, 3), across(3),
         own(1, 1), own(0, 1), own(1, 3), side(1, 1), side(1, 0), side(0, 1), side(1, 3), side(3, 1), across(0),
         own(2, 2), own(1, 2), own(2, 3), own(0, 2), side(2, 0), side(0, 2), side(2, 1), side(1, 2), side(2, 2),
         side(2, 3), side(3, 2), across(1), across(2),
-        make(half, same, half, far, 30), make(half + 1, same, half + 1, far, 31),
-        make(0, same, 2, far, 32), make(1, same, 3, far, 33),
+        make(half, back, half, near, 30), make(half + 1, back, half + 1, near, 31),
+        make(0, back, 2, near, 32), make(1, back, 3, near, 33),
     ]
 
 
@@ -111,42 +111,34 @@
     own_index = pltpu.make_async_copy(index_ref, indices.at[h], ts.at[3])
     own_index.start()
     comps = range(3)
-    to_hp = [send(x_ref.at[k, :, cells(hp)], blocks.at[y, h, k], zs.at[0, k], zr.at[0, k], dev_hp) for k in comps]
-    to_hm = [send(x_ref.at[k, :, cells(hm)], blocks.at[y, h, k], zs.at[1, k], zr.at[1, k], dev_hm) for k in comps]
-
-    moved, passed = {}, {}
+    to_hp, to_hm, via_hp, via_hm, on_hp, on_hm, moved = {}, {}, {}, {}, {}, {}, {}
+
+    def near(k):
+        to_hp[k] = send(x_ref.at[k, :, cells(hp)], blocks.at[y, h, k], zs.at[0, k], zr.at[0, k], dev_hp)
+        to_hm[k] = send(x_ref.at[k, :, cells(hm)], blocks.at[y, h, k], zs.at[1, k], zr.at[1, k], dev_hm)
+
+    def away(k):
+        via_hp[k] = send(x_ref.at[k, first_rows, cells(h2)], relay.at[0, k], zs.at[2, k], zr.at[2, k], dev_hp)
+        via_hm[k] = send(x_ref.at[k, last_rows, cells(h2)], relay.at[1, k], zs.at[3, k], zr.at[3, k], dev_hm)
 
     def spread(key, z, k, src=None):
         src = blocks.at[y, z, k] if src is None else src
-        dst = blocks.at[y, z, k]
-        moved[key, k, 0] = send(src, dst, ys.at[key, k, 0], yr.at[key, k, 0], dev_ym)
-        if k > 0:
-            moved[key, k, 1] = send(src, dst, ys.at[key, k, 1], yr.at[key, k, 1], dev_yp)
-
-    def forward(key, z, k):
-        if k == 0:
-            moved[key, k, 0].wait_recv()
-            block, peer = blocks.at[yp, z, k], dev_ym
-        else:
-            moved[key, k, 1].wait_recv()
-            block, peer = blocks.at[ym, z, k], dev_yp
-        passed[key, k] = send(block, block, ys.at[key, k, 2], yr.at[key, k, 2], peer)
+        for way, peer in enumerate((dev_yp, dev_ym)):
+            moved[key, k, way] = send(src, blocks.at[y, z, k], ys.at[key, k, way], yr.at[key, k, way], peer)
 
     def gathered(key):
         for k in comps:
-            if k > 0:
-                moved[key, k, 0].wait_recv()
-            passed[key, k].wait_recv()
-
+            for way in range(2):
+                moved[key, k, way].wait_recv()
+
+    near(0)
+    near(1)
     for k in comps:
         spread(0, h, k, x_ref.at[k, :, cells(h)])
-    via_hp = [send(x_ref.at[k, first_rows, cells(h2)], relay.at[0, k], zs.at[2, k], zr.at[2, k], dev_hp) for k in comps]
-    via_hm = [send(x_ref.at[k, last_rows, cells(h2)], relay.at[1, k], zs.at[3, k], zr.at[3, k], dev_hm) for k in comps]
     told = [
         send(index_ref, indices.at[h], ts.at[number], tr.at[number], peer)
         for number, peer in enumerate((dev_hp, dev_hm, dev_h2))
     ]
-    on_hp, on_hm = {}, {}
 
     def onward(k):
         via_hp[k].wait_recv()
@@ -230,42 +222,38 @@
             slot = begin + step
             total[pick(step, [tile[2] for tile in some])] = part[slot, core, x] + xlast[0, slot] + xlast[1, slot]
 
-    for k in comps:
-        forward(0, h, k)
-    for k in comps:
-        to_hp[k].wait_recv()
-        spread(1, hm, k)
+    to_hp[0].wait_recv()
+    spread(1, hm, 0)
     to_hm[0].wait_recv()
+    near(2)
+    to_hp[1].wait_recv()
+    spread(1, hm, 1)
+    to_hm[1].wait_recv()
+    away(0)
     spread(2, hp, 0)
-    forward(1, hm, 0)
-    forward(1, hm, 1)
-    to_hm[1].wait_recv()
+    to_hp[2].wait_recv()
+    spread(1, hm, 2)
+    to_hm[2].wait_recv()
+    away(1)
+    away(2)
     spread(2, hp, 1)
-    onward(0)
-    forward(1, hm, 2)
-    to_hm[2].wait_recv()
     spread(2, hp, 2)
-    onward(1)
-    onward(2)
-    forward(2, hp, 0)
-    forward(2, hp, 1)
     local.wait()
     gathered(0)
+    onward(0)
     gathered(1)
     pair0 = compute(0)
-    forward(2, hp, 2)
-    spread_far(0)
+    onward(1)
     first0 = add_pair(0, pair0)
-    spread_far(1)
+    onward(2)
     last0 = add_first(0, first0)
-    spread_far(2)
     gathered(2)
     pair1 = compute(1)
-    forward(3, h2, 0)
+    spread_far(0)
     first1 = add_pair(1, pair1)
-    forward(3, h2, 1)
+    spread_far(1)
     last1 = add_first(1, first1)
-    forward(3, h2, 2)
+    spread_far(2)
     add_last(0, last0)
     gathered(3)
     pair2 = compute(2)
@@ -398,7 +386,7 @@
             pltpu.VMEM((3, SLOTS, 8, 128), f32),
             pltpu.VMEM((2, SLOTS // 2, 8, 128), f32),
             pltpu.VMEM((3, SLOTS, 8, 128), f32),
-            dma(()), dma((6, 3)), dma((6, 3)), dma((4, 3, 3)), dma((4, 3, 3)), dma((count,)), dma((count,)),
+            dma(()), dma((6, 3)), dma((6, 3)), dma((4, 3, 2)), dma((4, 3, 2)), dma((count,)), dma((count,)),
             dma((count, 4)), dma((count, 4)), dma((2, 2, 4)), dma((2, 2, 4)),
             dma((4,)), dma((3,)), dma((2, 4)), dma((2, 4)), dma((6,)), dma((6,)),
         ],
@@ -417,7 +405,7 @@
     far_t = jnp.where(
         dz == 1, 26 + za, jnp.where(dz == 3, 26 + zb, jnp.where(dz == 0, 30 + za % 2, 32 + za))
     )
-    which_y = jnp.where(dy == 2, far_y, jnp.where(dy == 3, yb, ya))
+    which_y = jnp.where(dy == 2, (far_y + 1) % SIDE, jnp.where(dy == 3, yb, ya))
     which_t = jnp.where(
         dy == 0, own, jnp.where(dy == 1, 4 * za + zb, jnp.where(dy == 3, 4 * zb + za, far_t))
     )

time: 133 us -> 122 us (0.917)
  Pallas kernels: 130 us -> 118 us
    pallas_call x1, Pallas kernels: 130 us -> 118 us  [gram(): pl.pallas_call(lambda *refs: kernel(scale, *refs), out_shape=jax.ShapeDty...]
where the time goes in v4:
time: 122 us; the launch traced here: 121 us
  Pallas kernels  118 us (97%)
  local copies, waits for them, and re-layouts  2.33 us (2%)
    pallas_call x1, Pallas kernels, gram(): pl.pallas_call(lambda *refs: kernel(scale, *refs), out_shape=jax.ShapeDty...  118 us

profile of v4, /device:TPU:16, one launch (start us, length us, event | category | flops | bytes accessed | tf_op | source)
XLA Modules:
  0.0 121.1 jit_solution(15044204958068113582)
XLA Ops:
  0.0 0.8 compare_select_fusion.13
  0.8 0.6 broadcast_in_dim.8.refs_1_
  1.4 118.0 %gram_tiles.1 = f32[4,20,8,128]{3,2,1,0:T(8,128)} custom-call(bf16[3,256,1024]{2,1,0:T(8,128)(2,1)} %refs_0_.1, s32[8,128]{1,0:T(8,128)} %broadcast_in_dim.8.refs_1_), custom_call_target="tpu_custom_call" | custom-call | tf_op jit(solution)/shard_map/gram_tiles/pallas_call | solution.py:369
  119.4 1.7 %copy.5 = f32[20,2,8,2,128]{4,2,3,1,0:T(8,128)} copy(f32[20,2,8,2,128]{4,2,0,3,1:T(8,128)} %bitcast.34) | data formatting | bytes 655360 | tf_op jit(solution)/shard_map/transpose | solution.py:422
  (1 shorter events, 0.0 us)

commit v5 on v4

--- a/solution.py
+++ b/solution.py
@@ -12,8 +12,10 @@
 SIDE = 4
 SLOTS = 20
 TILES = 34
-BATCHES = (8, 9, 6, 6, 5)
-CHUNKS = ((0, 16), (16, 18))
+BATCHES = (7, 8, 6, 5, 8)
+NEAR, FAR = 26, 8
+CHUNKS = ((0, 14), (14, 12), (26, 4), (30, 4))
+SHARES = ((26, 8), (0, 14), (14, 12))
 
 
 def pick(index, values):
@@ -40,26 +42,22 @@
     def side(a, b):
         return make(z[a], same, z[b], near, SIDE * z[a] + z[b])
 
-    def across(a):
-        b = (a + 1) % SIDE
-        return make(z[a], back, z[b], near, 26 + z[a])
-
     half = jnp.where(back >= 2, 2, 0)
     return [
-        own(0, 0), side(0, 0),
-        own(3, 3), own(3, 0), side(0, 3), side(3, 0), side(3, 3), across(3),
-        own(1, 1), own(0, 1), own(1, 3), side(1, 1), side(1, 0), side(0, 1), side(1, 3), side(3, 1), across(0),
+        own(0, 0), side(0, 0), own(3, 3), own(3, 0), side(0, 3), side(3, 0), side(3, 3),
+        own(1, 1), own(0, 1), own(1, 3), side(1, 1), side(1, 0), side(0, 1), side(1, 3), side(3, 1),
         own(2, 2), own(1, 2), own(2, 3), own(0, 2), side(2, 0), side(0, 2), side(2, 1), side(1, 2), side(2, 2),
-        side(2, 3), side(3, 2), across(1), across(2),
+        side(2, 3), side(3, 2),
+        make(0, back, 1, near, 26), make(1, back, 2, near, 27), make(2, back, 3, near, 28), make(3, back, 0, near, 29),
         make(half, back, half, near, 30), make(half + 1, back, half + 1, near, 31),
         make(0, back, 2, near, 32), make(1, back, 3, near, 33),
     ]
 
 
 def kernel(
-    scale, x_ref, index_ref, out_ref, blocks, relay, part, pair, xfirst, xlast, total, zpart,
+    scale, x_ref, index_ref, out_ref, blocks, relay, part, pair, xfirst, xlast, total, zpart, zfar, zsum, xfar,
     indices, wanted, pieces, chosen, through, landed,
-    local_sem, zs, zr, ys, yr, ps, pr, xs, xr, ws, wr, ts, tr, gs, gr, os, onr,
+    local_sem, zs, zr, ys, yr, ps, pr, xs, xr, ws, wr, fs, fr, ts, tr, gs, gr, os, onr,
 ):
     tm, space = lax.axis_index("tm"), lax.axis_index("space")
     h, y = tm // SIDE, lax.rem(tm, SIDE)
@@ -189,6 +187,8 @@
         def _(slot):
             part[slot, core] = part[slot, core] + pair[slot]
 
+        if begin == NEAR:
+            return None
         span = pl.ds(begin, size)
         return (
             send(part.at[span, core, x2, pl.ds(0, 4)], xfirst.at[0, span], xs.at[number, 0], xr.at[number, 0], dev_xp),
@@ -221,6 +221,80 @@
         def _(step):
             slot = begin + step
             total[pick(step, [tile[2] for tile in some])] = part[slot, core, x] + xlast[0, slot] + xlast[1, slot]
+
+    def piece(step):
+        target = up(place, step, 8)
+        return lax.rem(target, 2) * 4 + target // 2
+
+    flying = {}
+
+    def pass_on(chunk, way, number):
+        begin, size = CHUNKS[chunk]
+        hops = 4 if chunk % 2 == way else 3
+        if number >= hops:
+            return
+        distance = hops - number
+        which = piece(distance if way == 0 else 8 - distance)
+        if begin < NEAR:
+            source, box, at, whole = total, zpart, (), ()
+        else:
+            source, box, at, whole = part, zfar, (core, every), (every,)
+        if number > 0:
+            flying[chunk, way].wait_recv()
+            old = box[(way, number - 1, pl.ds(begin % NEAR, size)) + whole]
+            where = (pl.ds(begin, size),) + at + (which,)
+            source[where] = source[where] + old
+        flying[chunk, way] = send(
+            source.at[(pl.ds(begin, size),) + at + (which,)], box.at[way, number, pl.ds(begin % NEAR, size)],
+            ws.at[chunk, way, number], wr.at[chunk, way, number], dev_zp if way == 0 else dev_zm,
+        )
+
+    def pass_all(chunks, number):
+        for first in range(2):
+            for chunk in chunks:
+                pass_on(chunk, (chunk + first) % 2, number)
+
+    def arrived(chunk):
+        for way in range(2):
+            flying[chunk, way].wait_recv()
+        return (3, 2) if chunk % 2 == 0 else (2, 3)
+
+    def far_sums():
+        for chunk in (2, 3):
+            begin, size = CHUNKS[chunk]
+            above, below = arrived(chunk)
+            here = begin - NEAR
+            zsum[here:here + size] = (
+                part[begin:begin + size, core, :, piece(0)]
+                + zfar[0, above, here:here + size] + zfar[1, below, here:here + size]
+            )
+        first, rest = pl.ds(0, FAR // 2), pl.ds(FAR // 2, FAR // 2)
+        return (
+            send(zsum.at[first, x2], xfar.at[0, 0, first], fs.at[0], fr.at[0], dev_xp),
+            send(zsum.at[rest, x2], xfar.at[0, 1, rest], fs.at[1], fr.at[1], dev_xm),
+        )
+
+    def far_cross(copies):
+        middle = FAR // 2
+        copies[0].wait_recv()
+        zsum[0:middle, xp] = zsum[0:middle, xp] + xfar[0, 0, 0:middle]
+        copies[1].wait_recv()
+        zsum[middle:FAR, xm] = zsum[middle:FAR, xm] + xfar[0, 1, middle:FAR]
+        return (
+            send(zsum.at[:, xp], xfar.at[1, 0], fs.at[2], fr.at[2], dev_xp),
+            send(zsum.at[:, xm], xfar.at[1, 1], fs.at[3], fr.at[3], dev_xm),
+        )
+
+    shared = {}
+
+    def share(number, value):
+        begin, size = SHARES[number]
+        span = pl.ds(y * TILES + begin, size)
+        pieces[span] = value * scale
+        shared[number] = (
+            send(pieces.at[span], pieces.at[span], gs.at[number, 0], gr.at[number, 0], dev_yp),
+            send(pieces.at[span], pieces.at[span], gs.at[number, 1], gr.at[number, 1], dev_ym),
+        )
 
     to_hp[0].wait_recv()
     spread(1, hm, 0)
@@ -255,67 +329,45 @@
     last1 = add_first(1, first1)
     spread_far(2)
     add_last(0, last0)
+    add_last(1, last1)
     gathered(3)
     pair2 = compute(2)
+    pair4 = compute(4)
+    first2 = add_pair(2, pair2)
     pair3 = compute(3)
-    first2 = add_pair(2, pair2)
-    pair4 = compute(4)
+    add_pair(4, pair4)
+    pass_all((2, 3), 0)
     first3 = add_pair(3, pair3)
-    add_last(1, last1)
-    first4 = add_pair(4, pair4)
     last2 = add_first(2, first2)
+    pass_all((2, 3), 1)
     last3 = add_first(3, first3)
-    last4 = add_first(4, first4)
+    pass_all((2, 3), 2)
     add_last(2, last2)
+    pass_all((2, 3), 3)
     add_last(3, last3)
-    add_last(4, last4)
-
-    def piece(step):
-        target = up(place, step, 8)
-        return lax.rem(target, 2) * 4 + target // 2
-
-    rings = ((0, 0, 4), (1, 1, 4), (0, 1, 3), (1, 0, 3))
-    flying = {}
-
-    def pass_on(chunk, way, hops, number):
-        begin, size = CHUNKS[chunk]
-        span = pl.ds(begin, size)
-        distance = hops - number
-        which = piece(distance if way == 0 else 8 - distance)
-        if number > 0:
-            flying[chunk, way].wait_recv()
-            total[begin:begin + size, which] = total[begin:begin + size, which] + zpart[way, number - 1, begin:begin + size]
-        flying[chunk, way] = send(
-            total.at[span, which], zpart.at[way, number, span],
-            ws.at[chunk, way, number], wr.at[chunk, way, number], dev_zp if way == 0 else dev_zm,
-        )
-
-    for number in range(4):
-        for chunk, way, hops in rings:
-            if number < hops:
-                pass_on(chunk, way, hops, number)
+    pass_all((0, 1), 0)
+    far = far_sums()
+    pass_all((0, 1), 1)
+    far = far_cross(far)
+    pass_all((0, 1), 2)
+    for copy in far:
+        copy.wait_recv()
+    share(0, zsum[:, x] + xfar[1, 0] + xfar[1, 1])
+    pass_all((0, 1), 3)
+    for chunk in range(2):
+        above, below = arrived(chunk)
+        begin, end = CHUNKS[chunk][0], sum(CHUNKS[chunk])
+        share(chunk + 1, total[begin:end, piece(0)] + zpart[0, above, begin:end] + zpart[1, below, begin:end])
 
     pieces[SIDE * TILES] = jnp.zeros((8, 128), jnp.float32)
-    shared, onto = {}, {}
-    for chunk, (begin, size) in enumerate(CHUNKS):
-        for way in range(2):
-            flying[chunk, way].wait_recv()
-        up_last, down_last = (3, 2) if chunk == 0 else (2, 3)
-        end = begin + size
-        value = total[begin:end, piece(0)] + zpart[0, up_last, begin:end] + zpart[1, down_last, begin:end]
-        span = pl.ds(y * TILES + begin, size)
-        pieces[span] = value * scale
-        shared[chunk] = (
-            send(pieces.at[span], pieces.at[span], gs.at[chunk, 0], gr.at[chunk, 0], dev_yp),
-            send(pieces.at[span], pieces.at[span], gs.at[chunk, 1], gr.at[chunk, 1], dev_ym),
-        )
+    onto = {}
     own_index.wait()
     for copy in told:
         copy.wait_recv()
     listed = pltpu.make_async_copy(indices, wanted, local_sem)
     listed.start()
     listed.wait()
-    for chunk, (begin, size) in enumerate(CHUNKS):
+    for chunk, (begin, size) in enumerate(SHARES):
         half = size // 2
         to_yp, to_ym = shared[chunk]
         to_yp.wait_recv()
@@ -325,7 +377,7 @@
         late = pl.ds(yp * TILES + begin + half, half)
         on_ym = send(pieces.at[late], pieces.at[late], gs.at[chunk, 3], gr.at[chunk, 3], dev_ym)
         onto[chunk] = (on_yp, on_ym)
-    for chunk in range(len(CHUNKS)):
+    for chunk in range(len(SHARES)):
         for copy in onto[chunk]:
             copy.wait_recv()
 
@@ -376,10 +428,13 @@
             pltpu.VMEM((2, 3, BLOCK // 2, BLOCK), b16),
             pltpu.VMEM((TILES, 2, 4, 8, 8, 128), f32),
             pltpu.VMEM((TILES, 4, 8, 8, 128), f32),
-            pltpu.VMEM((2, TILES, 4, 8, 128), f32),
-            pltpu.VMEM((2, TILES, 8, 8, 128), f32),
-            pltpu.VMEM((TILES, 8, 8, 128), f32),
-            pltpu.VMEM((2, 4, TILES, 8, 128), f32),
+            pltpu.VMEM((2, NEAR, 4, 8, 128), f32),
+            pltpu.VMEM((2, NEAR, 8, 8, 128), f32),
+            pltpu.VMEM((NEAR, 8, 8, 128), f32),
+            pltpu.VMEM((2, 4, NEAR, 8, 128), f32),
+            pltpu.VMEM((2, 4, FAR, 4, 8, 128), f32),
+            pltpu.VMEM((FAR, 4, 8, 128), f32),
+            pltpu.VMEM((2, 2, FAR, 8, 128), f32),
             pltpu.VMEM((SIDE, 8, 128), jnp.int32),
             pltpu.SMEM((SIDE, 8, 128), jnp.int32),
             pltpu.VMEM((SIDE * TILES + 1, 8, 128), f32),
@@ -387,8 +442,8 @@
             pltpu.VMEM((2, SLOTS // 2, 8, 128), f32),
             pltpu.VMEM((3, SLOTS, 8, 128), f32),
             dma(()), dma((6, 3)), dma((6, 3)), dma((4, 3, 2)), dma((4, 3, 2)), dma((count,)), dma((count,)),
-            dma((count, 4)), dma((count, 4)), dma((2, 2, 4)), dma((2, 2, 4)),
-            dma((4,)), dma((3,)), dma((2, 4)), dma((2, 4)), dma((6,)), dma((6,)),
+            dma((count, 4)), dma((count, 4)), dma((4, 2, 4)), dma((4, 2, 4)), dma((4,)), dma((4,)),
+            dma((4,)), dma((3,)), dma((3, 4)), dma((3, 4)), dma((6,)), dma((6,)),
         ],
         compiler_params=pltpu.CompilerParams(collective_id=0, has_side_effects=True, vmem_limit_bytes=60 * 2**20),
         name="gram_tiles",

time: 122 us -> 118 us (0.967)
  Pallas kernels: 118 us -> 113 us
    pallas_call x1, Pallas kernels: 118 us -> 113 us  [gram(): pl.pallas_call(lambda *refs: kernel(scale, *refs), out_shape=jax.ShapeDty...]
where the time goes in v5:
time: 118 us; the launch traced here: 116 us
  Pallas kernels  113 us (96%)
  local copies, waits for them, and re-layouts  2.33 us (2%)
    pallas_call x1, Pallas kernels, gram(): pl.pallas_call(lambda *refs: kernel(scale, *refs), out_shape=jax.ShapeDty...  113 us

profile of v5, /device:TPU:16, one launch (start us, length us, event | category | flops | bytes accessed | tf_op | source)
XLA Modules:
  0.0 116.2 jit_solution(5721931540972581689)
XLA Ops:
  0.0 0.8 compare_select_fusion.13
  0.8 0.6 broadcast_in_dim.8.refs_1_
  1.4 113.1 %gram_tiles.1 = f32[4,20,8,128]{3,2,1,0:T(8,128)} custom-call(bf16[3,256,1024]{2,1,0:T(8,128)(2,1)} %refs_0_.1, s32[8,128]{1,0:T(8,128)} %broadcast_in_dim.8.refs_1_), custom_call_target="tpu_custom_call" | custom-call | tf_op jit(solution)/shard_map/gram_tiles/pallas_call | solution.py:421
  114.5 1.7 %copy.5 = f32[20,2,8,2,128]{4,2,3,1,0:T(8,128)} copy(f32[20,2,8,2,128]{4,2,0,3,1:T(8,128)} %bitcast.34) | data formatting | bytes 655360 | tf_op jit(solution)/shard_map/transpose | solution.py:477
  (1 shorter events, 0.0 us)

commit v6 on v5

--- a/solution.py
+++ b/solution.py
@@ -12,17 +12,10 @@
 SIDE = 4
 SLOTS = 20
 TILES = 34
-BATCHES = (7, 8, 6, 5, 8)
+BATCHES = (2, 5, 8, 5, 6, 8)
 NEAR, FAR = 26, 8
 CHUNKS = ((0, 14), (14, 12), (26, 4), (30, 4))
 SHARES = ((26, 8), (0, 14), (14, 12))
-
-
-def pick(index, values):
-    chosen = values[0]
-    for place in range(1, len(values)):
-        chosen = jnp.where(index == place, values[place], chosen)
-    return chosen
 
 
 def tile_list(h, y):
@@ -42,15 +35,26 @@
     def side(a, b):
         return make(z[a], same, z[b], near, SIDE * z[a] + z[b])
 
+    def across(a):
+        return make(z[a], back, z[(a + 1) % SIDE], near, 26 + z[a])
+
+    def level(a):
+        return make(a, back, a, near, 30 + a - half)
+
+    def cross(a):
+        low = lax.rem(z[a], 2)
+        return make(low, back, low + 2, near, 32 + low)
+
     half = jnp.where(back >= 2, 2, 0)
+    early = jnp.where(z[2] == half, half + 1, half)
+    late = 2 * half + 1 - early
     return [
         own(0, 0), side(0, 0), own(3, 3), own(3, 0), side(0, 3), side(3, 0), side(3, 3),
         own(1, 1), own(0, 1), own(1, 3), side(1, 1), side(1, 0), side(0, 1), side(1, 3), side(3, 1),
         own(2, 2), own(1, 2), own(2, 3), own(0, 2), side(2, 0), side(0, 2), side(2, 1), side(1, 2), side(2, 2),
         side(2, 3), side(3, 2),
-        make(0, back, 1, near, 26), make(1, back, 2, near, 27), make(2, back, 3, near, 28), make(3, back, 0, near, 29),
-        make(half, back, half, near, 30), make(half + 1, back, half + 1, near, 31),
-        make(0, back, 2, near, 32), make(1, back, 3, near, 33),
+        across(0), across(3), cross(1), level(early),
+        across(1), across(2), cross(0), level(late),
     ]
 
 
@@ -152,14 +156,8 @@
     tiles = tile_list(h, y)
     starts = [sum(BATCHES[:number]) for number in range(len(BATCHES))]
 
-    def compute(number):
-        begin, size = starts[number], BATCHES[number]
-        some = tiles[begin:begin + size]
-
-        @pl.loop(0, size)
-        def _(step):
-            left = pick(step, [tile[0] for tile in some])
-            right = pick(step, [tile[1] for tile in some])
+    def compute(begin, size):
+        for slot, (left, right, tile) in enumerate(tiles[begin:begin + size], begin):
             ly, lz, ry, rz = left // SIDE, lax.rem(left, SIDE), right // SIDE, lax.rem(right, SIDE)
             product = None
             for comp in range(3):
@@ -168,7 +166,7 @@
                     preferred_element_type=jnp.float32,
                 )
                 product = term if product is None else product + term
-            slot = begin + step
+            slot = tile if slot >= NEAR else slot
             for row in range(BLOCK // 8):
                 for lane in range(2):
                     place_x, place_low, place_core, place_row = row // 8, row // 4 % 2, row // 2 % 2, row % 2
@@ -176,8 +174,13 @@
                         row * 8:row * 8 + 8, lane * 128:lane * 128 + 128
                     ]
 
-        span = pl.ds(begin, size)
+    def swap(number):
+        span = pl.ds(starts[number], BATCHES[number])
         return send(part.at[span, other], pair.at[span], ps.at[number], pr.at[number], dev_pair)
+
+    def begin_batch(number):
+        compute(starts[number], BATCHES[number])
+        return swap(number)
 
     def add_pair(number, copy):
         begin, size = starts[number], BATCHES[number]
@@ -215,12 +218,8 @@
         begin, size = starts[number], BATCHES[number]
         for copy in copies:
             copy.wait_recv()
-        some = tiles[begin:begin + size]
-
-        @pl.loop(0, size)
-        def _(step):
-            slot = begin + step
-            total[pick(step, [tile[2] for tile in some])] = part[slot, core, x] + xlast[0, slot] + xlast[1, slot]
+        for slot in range(begin, begin + size):
+            total[tiles[slot][2]] = part[slot, core, x] + xlast[0, slot] + xlast[1, slot]
 
     def piece(step):
         target = up(place, step, 8)
@@ -300,11 +299,16 @@
     spread(1, hm, 0)
     to_hm[0].wait_recv()
     near(2)
+    local.wait()
+    gathered(0)
+    pair0 = begin_batch(0)
     to_hp[1].wait_recv()
     spread(1, hm, 1)
     to_hm[1].wait_recv()
     away(0)
     spread(2, hp, 0)
+    first0 = add_pair(0, pair0)
+    last0 = add_first(0, first0)
     to_hp[2].wait_recv()
     spread(1, hm, 2)
     to_hm[2].wait_recv()
@@ -312,39 +316,40 @@
     away(2)
     spread(2, hp, 1)
     spread(2, hp, 2)
-    local.wait()
-    gathered(0)
     onward(0)
+    add_last(0, last0)
     gathered(1)
-    pair0 = compute(0)
+    pair1 = begin_batch(1)
     onward(1)
-    first0 = add_pair(0, pair0)
+    first1 = add_pair(1, pair1)
     onward(2)
-    last0 = add_first(0, first0)
     gathered(2)
-    pair1 = compute(1)
+    pair2 = begin_batch(2)
+    last1 = add_first(1, first1)
     spread_far(0)
-    first1 = add_pair(1, pair1)
+    first2 = add_pair(2, pair2)
     spread_far(1)
-    last1 = add_first(1, first1)
+    compute(NEAR, 4)
     spread_far(2)
-    add_last(0, last0)
+    last2 = add_first(2, first2)
     add_last(1, last1)
     gathered(3)
-    pair2 = compute(2)
-    pair4 = compute(4)
-    first2 = add_pair(2, pair2)
-    pair3 = compute(3)
-    add_pair(4, pair4)
+    pair3 = begin_batch(3)
+    compute(NEAR + 4, 4)
+    pair5 = swap(5)
+    pair4 = begin_batch(4)
+    first3 = add_pair(3, pair3)
+    add_pair(5, pair5)
     pass_all((2, 3), 0)
-    first3 = add_pair(3, pair3)
-    last2 = add_first(2, first2)
+    first4 = add_pair(4, pair4)
+    last3 = add_first(3, first3)
     pass_all((2, 3), 1)
-    last3 = add_first(3, first3)
+    last4 = add_first(4, first4)
+    add_last(2, last2)
     pass_all((2, 3), 2)
-    add_last(2, last2)
+    add_last(3, last3)
     pass_all((2, 3), 3)
-    add_last(3, last3)
+    add_last(4, last4)
     pass_all((0, 1), 0)
     far = far_sums()
     pass_all((0, 1), 1)

time: 118 us -> 107 us (0.907); the launches traced: 116 us -> 107 us
  Pallas kernels: 113 us -> 104 us
    pallas_call x1, Pallas kernels: 113 us -> 104 us  [gram(): pl.pallas_call(lambda *refs: kernel(scale, *refs), out_shape=jax.ShapeDty...]
where the time goes in v6:
time: 107 us
  Pallas kernels  104 us (97%)
  local copies, waits for them, and re-layouts  2.33 us (2%)
    pallas_call x1, Pallas kernels, gram(): pl.pallas_call(lambda *refs: kernel(scale, *refs), out_shape=jax.ShapeDty...  104 us

profile of v6, /device:TPU:16, one launch (start us, length us, event | category | flops | bytes accessed | tf_op | source)
XLA Modules:
  0.0 106.7 jit_solution(16156763326002349569)
XLA Ops:
  0.0 0.8 compare_select_fusion.13
  0.8 0.6 broadcast_in_dim.8.refs_1_
  1.4 103.6 %gram_tiles.1 = f32[4,20,8,128]{3,2,1,0:T(8,128)} custom-call(bf16[3,256,1024]{2,1,0:T(8,128)(2,1)} %refs_0_.1, s32[8,128]{1,0:T(8,128)} %broadcast_in_dim.8.refs_1_), custom_call_target="tpu_custom_call" | custom-call | tf_op jit(solution)/shard_map/gram_tiles/pallas_call | solution.py:426
  105.0 1.7 %copy.5 = f32[20,2,8,2,128]{4,2,3,1,0:T(8,128)} copy(f32[20,2,8,2,128]{4,2,0,3,1:T(8,128)} %bitcast.34) | data formatting | bytes 655360 | tf_op jit(solution)/shard_map/transpose | solution.py:482
  (1 shorter events, 0.0 us)

commit v7 on v6

--- a/solution.py
+++ b/solution.py
@@ -14,7 +14,7 @@
 TILES = 34
 BATCHES = (2, 5, 8, 5, 6, 8)
 NEAR, FAR = 26, 8
-CHUNKS = ((0, 14), (14, 12), (26, 4), (30, 4))
+CHUNKS = ((0, 7), (7, 7), (14, 6), (20, 6), (26, 4), (30, 4))
 SHARES = ((26, 8), (0, 14), (14, 12))
 
 
@@ -29,11 +29,12 @@
 
     def own(a, b):
         step = (b - a) % SIDE
-        base = lax.rem(z[a], 2) if step == 2 else z[a]
-        return make(z[a], same, z[b], same, 16 + 4 * step + base)
+        base = 12 + lax.rem(z[a], 2) if step == 2 else z[a] + (22 if step == 1 else 8)
+        return make(z[a], same, z[b], same, base)
 
     def side(a, b):
-        return make(z[a], same, z[b], near, SIDE * z[a] + z[b])
+        step = (b - a) % SIDE
+        return make(z[a], same, z[b], near, z[a] + (0, 4, 14, 18)[step])
 
     def across(a):
         return make(z[a], back, z[(a + 1) % SIDE], near, 26 + z[a])
@@ -51,15 +52,28 @@
     return [
         own(0, 0), side(0, 0), own(3, 3), own(3, 0), side(0, 3), side(3, 0), side(3, 3),
         own(1, 1), own(0, 1), own(1, 3), side(1, 1), side(1, 0), side(0, 1), side(1, 3), side(3, 1),
-        own(2, 2), own(1, 2), own(2, 3), own(0, 2), side(2, 0), side(0, 2), side(2, 1), side(1, 2), side(2, 2),
-        side(2, 3), side(3, 2),
+        own(2, 2), own(0, 2), side(2, 2), side(2, 3), side(1, 2),
+        own(1, 2), own(2, 3), side(2, 0), side(0, 2), side(2, 1), side(3, 2),
         across(0), across(3), cross(1), level(early),
         across(1), across(2), cross(0), level(late),
     ]
 
 
+def tile_index(a, b):
+    za, ya, zb, yb = a >> 2, a & 3, b >> 2, b & 3
+    dy, dz, back = (yb - ya) & 3, (zb - za) & 3, (za - zb) & 3
+    own = jnp.where(dz == 2, 12 + (za & 1), jnp.where(dz == 3, 22 + zb, za + jnp.where(dz == 1, 22, 8)))
+    right = za + 4 * dz + jnp.where(dz >= 2, 6, 0)
+    left = zb + 4 * back + jnp.where(back >= 2, 6, 0)
+    far_y = jnp.where((dz == 3) | ((dz == 0) & (za >= 2)), yb, ya)
+    far = jnp.where(dz == 1, 26 + za, jnp.where(dz == 3, 26 + zb, jnp.where(dz == 0, 30 + (za & 1), 32 + za)))
+    which_y = jnp.where(dy == 2, (far_y + 1) & 3, jnp.where(dy == 3, yb, ya))
+    which = jnp.where(dy == 0, own, jnp.where(dy == 1, right, jnp.where(dy == 3, left, far)))
+    return jnp.where(a >= 0, which_y * TILES + which, SIDE * TILES)
+
+
 def kernel(
-    scale, x_ref, index_ref, out_ref, blocks, relay, part, pair, xfirst, xlast, total, zpart, zfar, zsum, xfar,
+    scale, x_ref, table_ref, out_ref, blocks, relay, part, pair, xfirst, xlast, total, zpart, zfar, zsum, xfar,
     indices, wanted, pieces, chosen, through, landed,
     local_sem, zs, zr, ys, yr, ps, pr, xs, xr, ws, wr, fs, fr, ts, tr, gs, gr, os, onr,
 ):
@@ -79,7 +93,7 @@
     other = 1 - core
     place = h * 2 + low
     zp, zm = up(place, 1, 8), up(place, 7, 8)
-    dev_hp, dev_hm, dev_h2 = device(h_=hp), device(h_=hm), device(h_=h2)
+    dev_hp, dev_hm = device(h_=hp), device(h_=hm)
     dev_yp, dev_ym = device(y_=yp), device(y_=ym)
     dev_xp, dev_xm = device(x_=xp), device(x_=xm)
     dev_zp = device(h_=zp // 2, low_=lax.rem(zp, 2))
@@ -87,7 +101,7 @@
     dev_pair = device(core_=other)
 
     barrier = pltpu.get_barrier_semaphore()
-    peers = (dev_hp, dev_hm, dev_h2, dev_yp, dev_ym, dev_xp, dev_xm, dev_zp, dev_zm, dev_pair)
+    peers = (dev_hp, dev_hm, dev_yp, dev_ym, dev_xp, dev_xm, dev_zp, dev_zm, dev_pair)
     for peer in peers:
         pl.semaphore_signal(barrier, inc=1, device_id=peer, device_id_type=MESH)
     pl.semaphore_wait(barrier, len(peers))
@@ -110,8 +124,6 @@
 
     local = pltpu.make_async_copy(x_ref.at[:, :, cells(h)], blocks.at[y, h], local_sem)
     local.start()
-    own_index = pltpu.make_async_copy(index_ref, indices.at[h], ts.at[3])
-    own_index.start()
     comps = range(3)
     to_hp, to_hm, via_hp, via_hm, on_hp, on_hm, moved = {}, {}, {}, {}, {}, {}, {}
 
@@ -137,9 +149,11 @@
     near(1)
     for k in comps:
         spread(0, h, k, x_ref.at[k, :, cells(h)])
+    indices[h] = jnp.zeros((8, 128), jnp.int32)
+    indices[h, 0:1, 0:SLOTS] = tile_index(table_ref[0, 0:1, :], table_ref[0, 1:2, :])
     told = [
-        send(index_ref, indices.at[h], ts.at[number], tr.at[number], peer)
-        for number, peer in enumerate((dev_hp, dev_hm, dev_h2))
+        send(indices.at[h], indices.at[h], ts.at[number], tr.at[number], peer)
+        for number, peer in enumerate((dev_hp, dev_hm))
     ]
 
     def onward(k):
@@ -259,7 +273,7 @@
         return (3, 2) if chunk % 2 == 0 else (2, 3)
 
     def far_sums():
-        for chunk in (2, 3):
+        for chunk in (4, 5):
             begin, size = CHUNKS[chunk]
             above, below = arrived(chunk)
             here = begin - NEAR
@@ -294,6 +308,14 @@
             send(pieces.at[span], pieces.at[span], gs.at[number, 0], gr.at[number, 0], dev_yp),
             send(pieces.at[span], pieces.at[span], gs.at[number, 1], gr.at[number, 1], dev_ym),
         )
+
+    def share_near(number, chunks):
+        parts = []
+        for chunk in chunks:
+            above, below = arrived(chunk)
+            begin, end = CHUNKS[chunk][0], sum(CHUNKS[chunk])
+            parts.append(total[begin:end, piece(0)] + zpart[0, above, begin:end] + zpart[1, below, begin:end])
+        share(number, jnp.concatenate(parts))
 
     to_hp[0].wait_recv()
     spread(1, hm, 0)
@@ -318,6 +340,8 @@
     spread(2, hp, 2)
     onward(0)
     add_last(0, last0)
+    told[0].wait_recv()
+    told.append(send(indices.at[hm], indices.at[hm], ts.at[2], tr.at[2], dev_hp))
     gathered(1)
     pair1 = begin_batch(1)
     onward(1)
@@ -340,35 +364,36 @@
     pair4 = begin_batch(4)
     first3 = add_pair(3, pair3)
     add_pair(5, pair5)
-    pass_all((2, 3), 0)
+    pass_all((4, 5), 0)
     first4 = add_pair(4, pair4)
     last3 = add_first(3, first3)
+    pass_all((4, 5), 1)
+    add_last(2, last2)
+    last4 = add_first(4, first4)
+    pass_all((4, 5), 2)
+    add_last(3, last3)
+    pass_all((0, 1), 0)
+    pass_all((4, 5), 3)
+    pass_all((0, 1), 1)
+    add_last(4, last4)
+    pass_all((2, 3), 0)
+    far = far_sums()
+    pass_all((0, 1), 2)
     pass_all((2, 3), 1)
-    last4 = add_first(4, first4)
-    add_last(2, last2)
+    far = far_cross(far)
+    pass_all((0, 1), 3)
     pass_all((2, 3), 2)
-    add_last(3, last3)
-    pass_all((2, 3), 3)
-    add_last(4, last4)
-    pass_all((0, 1), 0)
-    far = far_sums()
-    pass_all((0, 1), 1)
-    far = far_cross(far)
-    pass_all((0, 1), 2)
     for copy in far:
         copy.wait_recv()
     share(0, zsum[:, x] + xfar[1, 0] + xfar[1, 1])
-    pass_all((0, 1), 3)
-    for chunk in range(2):
-        above, below = arrived(chunk)
-        begin, end = CHUNKS[chunk][0], sum(CHUNKS[chunk])
-        share(chunk + 1, total[begin:end, piece(0)] + zpart[0, above, begin:end] + zpart[1, below, begin:end])
+    share_near(1, (0, 1))
+    pass_all((2, 3), 3)
+    share_near(2, (2, 3))
 
     pieces[SIDE * TILES] = jnp.zeros((8, 128), jnp.float32)
     onto = {}
-    own_index.wait()
-    for copy in told:
-        copy.wait_recv()
+    told[1].wait_recv()
+    told[2].wait_recv()
     listed = pltpu.make_async_copy(indices, wanted, local_sem)
     listed.start()
     listed.wait()
@@ -404,29 +429,34 @@
     far_hm.wait_recv()
     last_hm = send(through.at[1], landed.at[2, pl.ds(half, half)], os.at[5], onr.at[5], dev_hm)
 
-    @pl.loop(0, SLOTS)
-    def _(slot):
-        out_ref[h, slot] = pieces[wanted[h, 0, slot]]
-
+    def put(z, slot, value):
+        rows, lanes = pl.multiple_of(z // 2 * 8, 8), pl.multiple_of(lax.rem(z, 2) * 128, 128)
+        out_ref[0, slot, pl.ds(rows, 8), pl.ds(lanes, 128)] = value
+
+    for slot in range(SLOTS):
+        put(h, slot, pieces[wanted[h, 0, slot]])
     out_hp.wait_recv()
-    out_ref[hm] = landed[0]
+    for slot in range(SLOTS):
+        put(hm, slot, landed[0, slot])
     out_hm.wait_recv()
-    out_ref[hp] = landed[1]
+    for slot in range(SLOTS):
+        put(hp, slot, landed[1, slot])
     last_hp.wait_recv()
     last_hm.wait_recv()
-    out_ref[h2] = landed[2]
+    for slot in range(SLOTS):
+        put(h2, slot, landed[2, slot])
     for copy in started:
         copy.wait_send()
 
 
-def gram(snapshots, index, scale):
+def gram(snapshots, table, scale):
     count = len(BATCHES)
     dma = pltpu.SemaphoreType.DMA
     f32, b16 = jnp.float32, jnp.bfloat16
     return pl.pallas_call(
         lambda *refs: kernel(scale, *refs),
-        out_shape=jax.ShapeDtypeStruct((SIDE, SLOTS, 8, 128), f32),
-        in_specs=[pl.BlockSpec(memory_space=pl.ANY)] * 2,
+        out_shape=jax.ShapeDtypeStruct((1, SLOTS, 16, BLOCK), f32),
+        in_specs=[pl.BlockSpec(memory_space=pl.ANY), pl.BlockSpec(memory_space=pltpu.VMEM)],
         out_specs=pl.BlockSpec(memory_space=pltpu.VMEM),
         scratch_shapes=[
             pltpu.VMEM((4, 4, 3, BLOCK, BLOCK), b16),
@@ -447,39 +477,17 @@
             pltpu.VMEM((2, SLOTS // 2, 8, 128), f32),
             pltpu.VMEM((3, SLOTS, 8, 128), f32),
             dma(()), dma((6, 3)), dma((6, 3)), dma((4, 3, 2)), dma((4, 3, 2)), dma((count,)), dma((count,)),
-            dma((count, 4)), dma((count, 4)), dma((4, 2, 4)), dma((4, 2, 4)), dma((4,)), dma((4,)),
-            dma((4,)), dma((3,)), dma((3, 4)), dma((3, 4)), dma((6,)), dma((6,)),
+            dma((count, 4)), dma((count, 4)), dma((6, 2, 4)), dma((6, 2, 4)), dma((4,)), dma((4,)),
+            dma((3,)), dma((3,)), dma((3, 4)), dma((3, 4)), dma((6,)), dma((6,)),
         ],
         compiler_params=pltpu.CompilerParams(collective_id=0, has_side_effects=True, vmem_limit_bytes=60 * 2**20),
         name="gram_tiles",
-    )(snapshots, index)
-
-
-def tile_index(table):
-    a, b = table[:, 0], table[:, 1]
-    za, ya, zb, yb = a // SIDE, a % SIDE, b // SIDE, b % SIDE
-    dy, dz = (yb - ya) % SIDE, (zb - za) % SIDE
-    own = jnp.where(dz == 2, 24 + za % 2, jnp.where(dz == 3, 20 + zb, 16 + 4 * dz + za))
-    low = za < 2
-    far_y = jnp.where(dz == 3, yb, jnp.where((dz == 0) & ~low, yb, ya))
-    far_t = jnp.where(
-        dz == 1, 26 + za, jnp.where(dz == 3, 26 + zb, jnp.where(dz == 0, 30 + za % 2, 32 + za))
-    )
-    which_y = jnp.where(dy == 2, (far_y + 1) % SIDE, jnp.where(dy == 3, yb, ya))
-    which_t = jnp.where(
-        dy == 0, own, jnp.where(dy == 1, 4 * za + zb, jnp.where(dy == 3, 4 * zb + za, far_t))
-    )
-    return jnp.where(a >= 0, which_y * TILES + which_t, SIDE * TILES)
+    )(snapshots, table)
 
 
 def per_device(snapshots, tile_table):
-    cells_dev = snapshots.shape[2]
-    scale = 1.0 / math.sqrt(3 * cells_dev * lax.axis_size("space"))
-    table = tile_table[0]
-    slots = table.shape[0]
-    index = jnp.broadcast_to(jnp.pad(tile_index(table), (0, 128 - slots)), (8, 128))
-    tiles = gram(snapshots, index, scale).reshape(2, 2, slots, 8, 128)
-    return tiles.transpose(2, 0, 3, 1, 4).reshape(1, slots, 16, BLOCK)
+    scale = 1.0 / math.sqrt(3 * snapshots.shape[2] * lax.axis_size("space"))
+    return gram(snapshots, jnp.transpose(tile_table, (0, 2, 1)), scale)
 
 
 def solution(mesh):

time: 107 us -> 106 us (level)
    transpose x1 -> x0, local copies, waits for them, and re-layouts: 1.73 us -> none  [per_device(): return tiles.transpose(2, 0, 3, 1, 4).reshape(1, slots, 16, BLOCK)]
    unnamed x0 -> x1, local copies, waits for them, and re-layouts: none -> 1.72 us
where the time goes in v7:
time: 106 us; the launch traced here: 105 us
  Pallas kernels  104 us (98%)
  local copies, waits for them, and re-layouts  1.72 us (2%)
    pallas_call x1, Pallas kernels, gram(): pl.pallas_call(lambda *refs: kernel(scale, *refs), out_shape=jax.ShapeDty...  104 us

profile of v7, /device:TPU:16, one launch (start us, length us, event | category | flops | bytes accessed | tf_op | source)
XLA Modules:
  0.0 105.5 jit_solution(5736850584428053491)
XLA Ops:
  0.0 103.8 %gram_tiles.1 = f32[1,20,16,256]{3,2,1,0:T(8,128)} custom-call(bf16[3,256,1024]{2,1,0:T(8,128)(2,1)} %refs_0_.1, s32[1,2,20]{2,1,0:T(2,128)} %bitcast.1), custom_call_target="tpu_custom_call" | custom-call | tf_op jit(solution)/shard_map/gram_tiles/pallas_call | solution.py:456
  103.8 1.7 %copy.4 = f32[1,20,16,256]{3,2,1,0:T(8,128)} copy(f32[1,20,16,256]{3,2,1,0:T(8,128)} %gram_tiles.1) | data formatting | bytes 655360

commit v8 on v7

--- a/solution.py
+++ b/solution.py
@@ -12,10 +12,10 @@
 SIDE = 4
 SLOTS = 20
 TILES = 34
-BATCHES = (2, 5, 8, 5, 6, 8)
-NEAR, FAR = 26, 8
-CHUNKS = ((0, 7), (7, 7), (14, 6), (20, 6), (26, 4), (30, 4))
-SHARES = ((26, 8), (0, 14), (14, 12))
+BATCHES = (1, 4, 8, 5, 6, 10)
+NEAR, FAR = 24, 10
+CHUNKS = ((0, 6), (6, 6), (12, 6), (18, 6), (24, 5), (29, 5))
+SHARES = ((24, 10), (0, 12), (12, 12))
 
 
 def tile_list(h, y):
@@ -29,51 +29,51 @@
 
     def own(a, b):
         step = (b - a) % SIDE
-        base = 12 + lax.rem(z[a], 2) if step == 2 else z[a] + (22 if step == 1 else 8)
-        return make(z[a], same, z[b], same, base)
+        return make(z[a], same, z[b], same, 24 + 4 * step + (lax.rem(z[a], 2) if step == 2 else z[a]))
 
     def side(a, b):
         step = (b - a) % SIDE
-        return make(z[a], same, z[b], near, z[a] + (0, 4, 14, 18)[step])
+        return make(z[a], same, z[b], near, z[a] + (0, 4, 12, 16)[step])
 
     def across(a):
-        return make(z[a], back, z[(a + 1) % SIDE], near, 26 + z[a])
+        return make(z[a], back, z[(a + 1) % SIDE], near, 8 + z[a])
 
     def level(a):
-        return make(a, back, a, near, 30 + a - half)
+        return make(a, back, a, near, 20 + a - half)
 
     def cross(a):
         low = lax.rem(z[a], 2)
-        return make(low, back, low + 2, near, 32 + low)
+        return make(low, back, low + 2, near, 22 + low)
 
     half = jnp.where(back >= 2, 2, 0)
     early = jnp.where(z[2] == half, half + 1, half)
     late = 2 * half + 1 - early
     return [
-        own(0, 0), side(0, 0), own(3, 3), own(3, 0), side(0, 3), side(3, 0), side(3, 3),
-        own(1, 1), own(0, 1), own(1, 3), side(1, 1), side(1, 0), side(0, 1), side(1, 3), side(3, 1),
-        own(2, 2), own(0, 2), side(2, 2), side(2, 3), side(1, 2),
-        own(1, 2), own(2, 3), side(2, 0), side(0, 2), side(2, 1), side(3, 2),
-        across(0), across(3), cross(1), level(early),
-        across(1), across(2), cross(0), level(late),
+        side(0, 0),
+        side(0, 3), side(3, 0), side(3, 3), across(3),
+        side(1, 1), side(1, 0), side(0, 1), side(1, 3), side(3, 1), across(0), cross(1), level(early),
+        side(2, 2), side(2, 3), side(1, 2), across(1), across(2),
+        side(2, 0), side(0, 2), side(2, 1), side(3, 2), cross(0), level(late),
+        own(0, 0), own(3, 3), own(3, 0), own(1, 1), own(0, 1), own(1, 3),
+        own(2, 2), own(1, 2), own(2, 3), own(0, 2),
     ]
 
 
 def tile_index(a, b):
     za, ya, zb, yb = a >> 2, a & 3, b >> 2, b & 3
     dy, dz, back = (yb - ya) & 3, (zb - za) & 3, (za - zb) & 3
-    own = jnp.where(dz == 2, 12 + (za & 1), jnp.where(dz == 3, 22 + zb, za + jnp.where(dz == 1, 22, 8)))
-    right = za + 4 * dz + jnp.where(dz >= 2, 6, 0)
-    left = zb + 4 * back + jnp.where(back >= 2, 6, 0)
+    own = 24 + jnp.where(dz == 2, 8 + (za & 1), jnp.where(dz == 3, 4 + zb, za + 4 * dz))
+    right = za + 4 * dz + jnp.where(dz >= 2, 4, 0)
+    left = zb + 4 * back + jnp.where(back >= 2, 4, 0)
     far_y = jnp.where((dz == 3) | ((dz == 0) & (za >= 2)), yb, ya)
-    far = jnp.where(dz == 1, 26 + za, jnp.where(dz == 3, 26 + zb, jnp.where(dz == 0, 30 + (za & 1), 32 + za)))
+    far = jnp.where(dz == 1, 8 + za, jnp.where(dz == 3, 8 + zb, jnp.where(dz == 0, 20 + (za & 1), 22 + za)))
     which_y = jnp.where(dy == 2, (far_y + 1) & 3, jnp.where(dy == 3, yb, ya))
     which = jnp.where(dy == 0, own, jnp.where(dy == 1, right, jnp.where(dy == 3, left, far)))
     return jnp.where(a >= 0, which_y * TILES + which, SIDE * TILES)
 
 
 def kernel(
-    scale, x_ref, table_ref, out_ref, blocks, relay, part, pair, xfirst, xlast, total, zpart, zfar, zsum, xfar,
+    x_ref, table_ref, out_ref, blocks, relay, part, pair, xfirst, xlast, total, zpart, zfar, zsum, xfar,
     indices, wanted, pieces, chosen, through, landed,
     local_sem, zs, zr, ys, yr, ps, pr, xs, xr, ws, wr, fs, fr, ts, tr, gs, gr, os, onr,
 ):
@@ -248,24 +248,22 @@
             return
         distance = hops - number
         which = piece(distance if way == 0 else 8 - distance)
-        if begin < NEAR:
-            source, box, at, whole = total, zpart, (), ()
-        else:
-            source, box, at, whole = part, zfar, (core, every), (every,)
+        span, here = pl.ds(begin, size), pl.ds(begin - NEAR, size)
         if number > 0:
             flying[chunk, way].wait_recv()
-            old = box[(way, number - 1, pl.ds(begin % NEAR, size)) + whole]
-            where = (pl.ds(begin, size),) + at + (which,)
-            source[where] = source[where] + old
+            part[span, core, :, which] = part[span, core, :, which] + zfar[way, number - 1, here]
         flying[chunk, way] = send(
-            source.at[(pl.ds(begin, size),) + at + (which,)], box.at[way, number, pl.ds(begin % NEAR, size)],
+            part.at[span, core, :, which], zfar.at[way, number, here],
             ws.at[chunk, way, number], wr.at[chunk, way, number], dev_zp if way == 0 else dev_zm,
         )
+
+    def pass_some(chunks, first, number):
+        for chunk in chunks:
+            pass_on(chunk, (chunk + first) % 2, number)
 
     def pass_all(chunks, number):
         for first in range(2):
-            for chunk in chunks:
-                pass_on(chunk, (chunk + first) % 2, number)
+            pass_some(chunks, first, number)
 
     def arrived(chunk):
         for way in range(2):
@@ -303,18 +301,55 @@
     def share(number, value):
         begin, size = SHARES[number]
         span = pl.ds(y * TILES + begin, size)
-        pieces[span] = value * scale
+        pieces[span] = value
         shared[number] = (
             send(pieces.at[span], pieces.at[span], gs.at[number, 0], gr.at[number, 0], dev_yp),
             send(pieces.at[span], pieces.at[span], gs.at[number, 1], gr.at[number, 1], dev_ym),
         )
 
+    next_by, next_two = (dev_zp, dev_zm), (dev_hp, dev_hm)
+
+    def step_on(chunk, way, kind, distance, peer):
+        span = pl.ds(*CHUNKS[chunk])
+        which = piece(distance if way == 0 else 8 - distance)
+        flying[chunk, way, kind] = send(
+            total.at[span, which], zpart.at[way, kind, span], ws.at[chunk, way, kind], wr.at[chunk, way, kind], peer
+        )
+
+    def launch(chunks):
+        for chunk in chunks:
+            way = chunk % 2
+            step_on(chunk, way, 0, 4, next_two[way])
+        for chunk in chunks:
+            for way in range(2):
+                step_on(chunk, way, 1, 3, next_by[way])
+        for chunk in chunks:
+            for way in range(2):
+                step_on(chunk, way, 2, 1, next_by[way])
+
+    def meet(chunks):
+        for chunk in chunks:
+            begin, end = CHUNKS[chunk][0], sum(CHUNKS[chunk])
+            for way in (1 - chunk % 2, chunk % 2):
+                which = piece(2 if way == 0 else 6)
+                flying[chunk, way, 1].wait_recv()
+                added = total[begin:end, which] + zpart[way, 1, begin:end]
+                if chunk % 2 == way:
+                    flying[chunk, way, 0].wait_recv()
+                    added = added + zpart[way, 0, begin:end]
+                total[begin:end, which] = added
+                step_on(chunk, way, 3, 2, next_two[way])
+
     def share_near(number, chunks):
         parts = []
         for chunk in chunks:
-            above, below = arrived(chunk)
             begin, end = CHUNKS[chunk][0], sum(CHUNKS[chunk])
-            parts.append(total[begin:end, piece(0)] + zpart[0, above, begin:end] + zpart[1, below, begin:end])
+            value = total[begin:end, piece(0)]
+            for kind in (2, 3):
+                for way in range(2):
+                    flying[chunk, way, kind].wait_recv()
+                    value = value + zpart[way, kind, begin:end]
+            parts.append(value)
         share(number, jnp.concatenate(parts))
 
     to_hp[0].wait_recv()
@@ -353,41 +388,39 @@
     spread_far(0)
     first2 = add_pair(2, pair2)
     spread_far(1)
-    compute(NEAR, 4)
+    compute(NEAR, 6)
     spread_far(2)
+    compute(NEAR + 6, 4)
+    pair5 = swap(5)
     last2 = add_first(2, first2)
+    add_pair(5, pair5)
+    pass_all((4, 5), 0)
     add_last(1, last1)
     gathered(3)
     pair3 = begin_batch(3)
-    compute(NEAR + 4, 4)
-    pair5 = swap(5)
     pair4 = begin_batch(4)
+    pass_some((4, 5), 0, 1)
     first3 = add_pair(3, pair3)
-    add_pair(5, pair5)
-    pass_all((4, 5), 0)
+    pass_some((4, 5), 1, 1)
     first4 = add_pair(4, pair4)
+    pass_some((4, 5), 0, 2)
     last3 = add_first(3, first3)
-    pass_all((4, 5), 1)
+    pass_some((4, 5), 1, 2)
+    last4 = add_first(4, first4)
     add_last(2, last2)
-    last4 = add_first(4, first4)
-    pass_all((4, 5), 2)
+    pass_some((4, 5), 0, 3)
     add_last(3, last3)
-    pass_all((0, 1), 0)
-    pass_all((4, 5), 3)
-    pass_all((0, 1), 1)
+    launch((0, 1))
+    far = far_sums()
+    meet((0, 1))
     add_last(4, last4)
-    pass_all((2, 3), 0)
-    far = far_sums()
-    pass_all((0, 1), 2)
-    pass_all((2, 3), 1)
+    launch((2, 3))
     far = far_cross(far)
-    pass_all((0, 1), 3)
-    pass_all((2, 3), 2)
+    meet((2, 3))
     for copy in far:
         copy.wait_recv()
     share(0, zsum[:, x] + xfar[1, 0] + xfar[1, 1])
     share_near(1, (0, 1))
-    pass_all((2, 3), 3)
     share_near(2, (2, 3))
 
     pieces[SIDE * TILES] = jnp.zeros((8, 128), jnp.float32)
@@ -449,12 +482,12 @@
         copy.wait_send()
 
 
-def gram(snapshots, table, scale):
+def gram(snapshots, table):
     count = len(BATCHES)
     dma = pltpu.SemaphoreType.DMA
     f32, b16 = jnp.float32, jnp.bfloat16
     return pl.pallas_call(
-        lambda *refs: kernel(scale, *refs),
+        kernel,
         out_shape=jax.ShapeDtypeStruct((1, SLOTS, 16, BLOCK), f32),
         in_specs=[pl.BlockSpec(memory_space=pl.ANY), pl.BlockSpec(memory_space=pltpu.VMEM)],
         out_specs=pl.BlockSpec(memory_space=pltpu.VMEM),
@@ -487,7 +520,7 @@
 
 def per_device(snapshots, tile_table):
     scale = 1.0 / math.sqrt(3 * snapshots.shape[2] * lax.axis_size("space"))
-    return gram(snapshots, jnp.transpose(tile_table, (0, 2, 1)), scale)
+    return gram(snapshots, jnp.transpose(tile_table, (0, 2, 1))) * scale
 
 
 def solution(mesh):

time: 106 us -> 102 us (0.962); the launches traced: 105 us -> 100 us
  Pallas kernels: 104 us -> 98.7 us
  other arithmetic: 0 us -> 1.73 us
  local copies, waits for them, and re-layouts: 1.72 us -> 0 us
    pallas_call x1, Pallas kernels: 104 us -> 98.7 us  [gram(): pl.pallas_call(kernel, out_shape=jax.ShapeDtypeStruct((1, SLOTS, 16, BLOC...]
    mul x0 -> x1, other arithmetic: none -> 1.73 us  [per_device(): return gram(snapshots, jnp.transpose(tile_table, (0, 2, 1))) * scale]
    unnamed x1 -> x0, local copies, waits for them, and re-layouts: 1.72 us -> none
where the time goes in v8:
time: 102 us; the launch traced here: 100 us
  Pallas kernels  98.7 us (97%)
  other arithmetic  1.73 us (2%)
    pallas_call x1, Pallas kernels, gram(): pl.pallas_call(kernel, out_shape=jax.ShapeDtypeStruct((1, SLOTS, 16, BLOC...  98.7 us

profile of v8, /device:TPU:16, one launch (start us, length us, event | category | flops | bytes accessed | tf_op | source)
XLA Modules:
  0.0 100.4 jit_solution(7878892145431804516)
XLA Ops:
  0.0 98.7 %gram_tiles.1 = f32[1,20,16,256]{3,2,1,0:T(8,128)} custom-call(bf16[3,256,1024]{2,1,0:T(8,128)(2,1)} %x_ref.1, s32[1,2,20]{2,1,0:T(2,128)} %bitcast.1), custom_call_target="tpu_custom_call" | custom-call | tf_op jit(solution)/shard_map/gram_tiles/pallas_call | solution.py:489
  98.7 1.7 %broadcast_multiply_fusion = f32[1,20,16,256]{3,2,1,0:T(8,128)} fusion(f32[1,20,16,256]{3,2,1,0:T(8,128)} %gram_tiles.1), kind=kLoop, calls=%fused_computation | loop fusion | flops 81920 | bytes 655360 | tf_op jit(solution)/shard_map/mul | solution.py:523

commit v9 on v8

--- a/solution.py
+++ b/solution.py
@@ -101,7 +101,7 @@
     dev_pair = device(core_=other)
 
     barrier = pltpu.get_barrier_semaphore()
-    peers = (dev_hp, dev_hm, dev_yp, dev_ym, dev_xp, dev_xm, dev_zp, dev_zm, dev_pair)
+    peers = (dev_hp, dev_hm, device(y_=up(y, 2)), dev_yp, dev_ym, dev_xp, dev_xm, dev_zp, dev_zm, dev_pair)
     for peer in peers:
         pl.semaphore_signal(barrier, inc=1, device_id=peer, device_id_type=MESH)
     pl.semaphore_wait(barrier, len(peers))
@@ -396,17 +396,21 @@
     add_pair(5, pair5)
     pass_all((4, 5), 0)
     add_last(1, last1)
+    told[1].wait_recv()
+    told[2].wait_recv()
+    listed = pltpu.make_async_copy(indices, wanted, local_sem)
+    listed.start()
     gathered(3)
     pair3 = begin_batch(3)
     pair4 = begin_batch(4)
+    first3 = add_pair(3, pair3)
     pass_some((4, 5), 0, 1)
-    first3 = add_pair(3, pair3)
+    first4 = add_pair(4, pair4)
     pass_some((4, 5), 1, 1)
-    first4 = add_pair(4, pair4)
+    last3 = add_first(3, first3)
     pass_some((4, 5), 0, 2)
-    last3 = add_first(3, first3)
+    last4 = add_first(4, first4)
     pass_some((4, 5), 1, 2)
-    last4 = add_first(4, first4)
     add_last(2, last2)
     pass_some((4, 5), 0, 3)
     add_last(3, last3)
@@ -422,17 +426,19 @@
     share(0, zsum[:, x] + xfar[1, 0] + xfar[1, 1])
     share_near(1, (0, 1))
     share_near(2, (2, 3))
+    last = pl.ds(y * TILES + SHARES[2][0], SHARES[2][1])
+    across_y = send(pieces.at[last], pieces.at[last], gs.at[2, 2], gr.at[2, 2], device(y_=up(y, 2)))
 
     pieces[SIDE * TILES] = jnp.zeros((8, 128), jnp.float32)
     onto = {}
-    told[1].wait_recv()
-    told[2].wait_recv()
-    listed = pltpu.make_async_copy(indices, wanted, local_sem)
-    listed.start()
-    listed.wait()
     for chunk, (begin, size) in enumerate(SHARES):
         half = size // 2
         to_yp, to_ym = shared[chunk]
+        if chunk == 2:
+            to_yp.wait_recv()
+            to_ym.wait_recv()
+            onto[chunk] = (across_y,)
+            continue
         to_yp.wait_recv()
         early = pl.ds(ym * TILES + begin, half)
         on_yp = send(pieces.at[early], pieces.at[early], gs.at[chunk, 2], gr.at[chunk, 2], dev_yp)
@@ -444,9 +450,10 @@
         for copy in onto[chunk]:
             copy.wait_recv()
 
+    listed.wait()
+
     def choose(number, z):
-        @pl.loop(0, SLOTS)
-        def _(slot):
+        for slot in range(SLOTS):
             chosen[number, slot] = pieces[wanted[z, 0, slot]]
 
     half = SLOTS // 2
@@ -489,7 +496,7 @@
     return pl.pallas_call(
         kernel,
         out_shape=jax.ShapeDtypeStruct((1, SLOTS, 16, BLOCK), f32),
-        in_specs=[pl.BlockSpec(memory_space=pl.ANY), pl.BlockSpec(memory_space=pltpu.VMEM)],
+        in_specs=[pl.BlockSpec(memory_space=pltpu.HBM), pl.BlockSpec(memory_space=pltpu.VMEM)],
         out_specs=pl.BlockSpec(memory_space=pltpu.VMEM),
         scratch_shapes=[
             pltpu.VMEM((4, 4, 3, BLOCK, BLOCK), b16),
@@ -513,7 +520,7 @@
             dma((count, 4)), dma((count, 4)), dma((6, 2, 4)), dma((6, 2, 4)), dma((4,)), dma((4,)),
             dma((3,)), dma((3,)), dma((3, 4)), dma((3, 4)), dma((6,)), dma((6,)),
         ],
-        compiler_params=pltpu.CompilerParams(collective_id=0, has_side_effects=True, vmem_limit_bytes=60 * 2**20),
+        compiler_params=pltpu.CompilerParams(collective_id=0, has_side_effects=True, vmem_limit_bytes=30 * 2**20),
         name="gram_tiles",
     )(snapshots, table)
 

time: 102 us -> 99.6 us (0.976)
  Pallas kernels: 98.7 us -> 95.5 us
  local copies, waits for them, and re-layouts: 0 us -> 2.09 us
    pallas_call x1, Pallas kernels: 98.7 us -> 95.5 us  [gram(): pl.pallas_call(kernel, out_shape=jax.ShapeDtypeStruct((1, SLOTS, 16, BLOC...]
    unnamed x0 -> x4, local copies, waits for them, and re-layouts: none -> 2.09 us
where the time goes in v9:
time: 99.6 us; the launch traced here: 98.4 us
  Pallas kernels  95.5 us (96%)
  local copies, waits for them, and re-layouts  2.09 us (2%)
    pallas_call x1, Pallas kernels, gram(): pl.pallas_call(kernel, out_shape=jax.ShapeDtypeStruct((1, SLOTS, 16, BLOC...  95.5 us
    unnamed x4, local copies, waits for them, and re-layouts  2.09 us

profile of v9, /device:TPU:16, one launch (start us, length us, event | category | flops | bytes accessed | tf_op | source)
XLA Modules:
  0.0 98.4 jit_solution(1346349812125298445)
XLA Ops:
  0.0 0.0 copy-start
  0.0 1.4 %copy-done = bf16[3,256,1024]{2,1,0:T(8,128)(2,1)S(1)} copy-done((bf16[3,256,1024]{2,1,0:T(8,128)(2,1)S(1)}, bf16[3,256,1024]{2,1,0:T(8,128)(2,1)}, u32[]{:S(2)}) %copy-start) | copy-done | bytes 1572888
  1.4 0.0 copy-start.1
  1.4 0.7 copy-done.1
  2.1 95.5 %gram_tiles.1 = f32[1,20,16,256]{3,2,1,0:T(8,128)S(1)} custom-call(bf16[3,256,1024]{2,1,0:T(8,128)(2,1)S(1)} %copy-done, s32[1,2,20]{2,1,0:T(2,128)S(1)} %bitcast.1), custom_call_target="tpu_custom_call" | custom-call | tf_op jit(solution)/shard_map/gram_tiles/pallas_call | solution.py:496
  97.6 0.8 broadcast_multiply_fusion
Async XLA Ops:
  0.0 1.4 %copy-start = (bf16[3,256,1024]{2,1,0:T(8,128)(2,1)S(1)}, bf16[3,256,1024]{2,1,0:T(8,128)(2,1)}, u32[]{:S(2)}) copy-start(bf16[3,256,1024]{2,1,0:T(8,128)(2,1)} %x_ref.1) | copy-start | bytes 4718596
  1.4 0.7 copy-start.1

commit v10 on v9

--- a/solution.py
+++ b/solution.py
@@ -101,7 +101,7 @@
     dev_pair = device(core_=other)
 
     barrier = pltpu.get_barrier_semaphore()
-    peers = (dev_hp, dev_hm, device(y_=up(y, 2)), dev_yp, dev_ym, dev_xp, dev_xm, dev_zp, dev_zm, dev_pair)
+    peers = (dev_hp, dev_hm, device(h_=h2), device(y_=up(y, 2)), dev_yp, dev_ym, dev_xp, dev_xm, dev_zp, dev_zm, dev_pair)
     for peer in peers:
         pl.semaphore_signal(barrier, inc=1, device_id=peer, device_id_type=MESH)
     pl.semaphore_wait(barrier, len(peers))
@@ -296,7 +296,7 @@
             send(zsum.at[:, xm], xfar.at[1, 1], fs.at[3], fr.at[3], dev_xm),
         )
 
-    shared = {}
+    shared, across_y = {}, {}
 
     def share(number, value):
         begin, size = SHARES[number]
@@ -351,6 +351,11 @@
                     value = value + zpart[way, kind, begin:end]
             parts.append(value)
         share(number, jnp.concatenate(parts))
+        begin, size = SHARES[number]
+        span = pl.ds(y * TILES + begin, size)
+        across_y[number] = send(
+            pieces.at[span], pieces.at[span], gs.at[number, 2], gr.at[number, 2], device(y_=up(y, 2))
+        )
 
     to_hp[0].wait_recv()
     spread(1, hm, 0)
@@ -426,18 +431,16 @@
     share(0, zsum[:, x] + xfar[1, 0] + xfar[1, 1])
     share_near(1, (0, 1))
     share_near(2, (2, 3))
-    last = pl.ds(y * TILES + SHARES[2][0], SHARES[2][1])
-    across_y = send(pieces.at[last], pieces.at[last], gs.at[2, 2], gr.at[2, 2], device(y_=up(y, 2)))
 
     pieces[SIDE * TILES] = jnp.zeros((8, 128), jnp.float32)
     onto = {}
     for chunk, (begin, size) in enumerate(SHARES):
         half = size // 2
         to_yp, to_ym = shared[chunk]
-        if chunk == 2:
+        if chunk > 0:
             to_yp.wait_recv()
             to_ym.wait_recv()
-            onto[chunk] = (across_y,)
+            onto[chunk] = (across_y[chunk],)
             continue
         to_yp.wait_recv()
         early = pl.ds(ym * TILES + begin, half)
@@ -458,16 +461,12 @@
 
     half = SLOTS // 2
     choose(2, h2)
-    far_hp = send(chosen.at[2, pl.ds(0, half)], through.at[0], os.at[2], onr.at[2], dev_hp)
-    far_hm = send(chosen.at[2, pl.ds(half, half)], through.at[1], os.at[3], onr.at[3], dev_hm)
+    last_hp = send(chosen.at[2, pl.ds(0, half)], landed.at[2, pl.ds(0, half)], os.at[2], onr.at[2], device(h_=h2))
+    last_hm = send(chosen.at[2, pl.ds(half, half)], landed.at[2, pl.ds(half, half)], os.at[3], onr.at[3], device(h_=h2))
     choose(0, hp)
     out_hp = send(chosen.at[0], landed.at[0], os.at[0], onr.at[0], dev_hp)
     choose(1, hm)
     out_hm = send(chosen.at[1], landed.at[1], os.at[1], onr.at[1], dev_hm)
-    far_hp.wait_recv()
-    last_hp = send(through.at[0], landed.at[2, pl.ds(0, half)], os.at[4], onr.at[4], dev_hp)
-    far_hm.wait_recv()
-    last_hm = send(through.at[1], landed.at[2, pl.ds(half, half)], os.at[5], onr.at[5], dev_hm)
 
     def put(z, slot, value):
         rows, lanes = pl.multiple_of(z // 2 * 8, 8), pl.multiple_of(lax.rem(z, 2) * 128, 128)

time: 99.6 us -> 98.3 us (0.987)
  Pallas kernels: 95.5 us -> 94.4 us
    pallas_call x1, Pallas kernels: 95.5 us -> 94.4 us  [gram(): pl.pallas_call(kernel, out_shape=jax.ShapeDtypeStruct((1, SLOTS, 16, BLOC...]
where the time goes in v10:
time: 98.3 us; the launch traced here: 97.2 us
  Pallas kernels  94.4 us (96%)
  local copies, waits for them, and re-layouts  2.09 us (2%)
    pallas_call x1, Pallas kernels, gram(): pl.pallas_call(kernel, out_shape=jax.ShapeDtypeStruct((1, SLOTS, 16, BLOC...  94.4 us
    unnamed x4, local copies, waits for them, and re-layouts  2.09 us

profile of v10, /device:TPU:16, one launch (start us, length us, event | category | flops | bytes accessed | tf_op | source)
XLA Modules:
  0.0 97.2 jit_solution(10752744026496975057)
XLA Ops:
  0.0 0.0 copy-start
  0.0 1.4 %copy-done = bf16[3,256,1024]{2,1,0:T(8,128)(2,1)S(1)} copy-done((bf16[3,256,1024]{2,1,0:T(8,128)(2,1)S(1)}, bf16[3,256,1024]{2,1,0:T(8,128)(2,1)}, u32[]{:S(2)}) %copy-start) | copy-done | bytes 1572888
  1.4 0.0 copy-start.1
  1.4 0.7 copy-done.1
  2.1 94.4 %gram_tiles.1 = f32[1,20,16,256]{3,2,1,0:T(8,128)S(1)} custom-call(bf16[3,256,1024]{2,1,0:T(8,128)(2,1)S(1)} %copy-done, s32[1,2,20]{2,1,0:T(2,128)S(1)} %bitcast.1), custom_call_target="tpu_custom_call" | custom-call | tf_op jit(solution)/shard_map/gram_tiles/pallas_call | solution.py:495
  96.5 0.8 broadcast_multiply_fusion
Async XLA Ops:
  0.0 1.4 %copy-start = (bf16[3,256,1024]{2,1,0:T(8,128)(2,1)S(1)}, bf16[3,256,1024]{2,1,0:T(8,128)(2,1)}, u32[]{:S(2)}) copy-start(bf16[3,256,1024]{2,1,0:T(8,128)(2,1)} %x_ref.1) | copy-start | bytes 4718596
  1.4 0.7 copy-start.1

commit v11 on v10

--- a/solution.py
+++ b/solution.py
@@ -306,6 +306,9 @@
             send(pieces.at[span], pieces.at[span], gs.at[number, 0], gr.at[number, 0], dev_yp),
             send(pieces.at[span], pieces.at[span], gs.at[number, 1], gr.at[number, 1], dev_ym),
         )
+        across_y[number] = send(
+            pieces.at[span], pieces.at[span], gs.at[number, 2], gr.at[number, 2], device(y_=up(y, 2))
+        )
 
     next_by, next_two = (dev_zp, dev_zm), (dev_hp, dev_hm)
 
@@ -351,11 +354,6 @@
                     value = value + zpart[way, kind, begin:end]
             parts.append(value)
         share(number, jnp.concatenate(parts))
-        begin, size = SHARES[number]
-        span = pl.ds(y * TILES + begin, size)
-        across_y[number] = send(
-            pieces.at[span], pieces.at[span], gs.at[number, 2], gr.at[number, 2], device(y_=up(y, 2))
-        )
 
     to_hp[0].wait_recv()
     spread(1, hm, 0)
@@ -433,26 +431,9 @@
     share_near(2, (2, 3))
 
     pieces[SIDE * TILES] = jnp.zeros((8, 128), jnp.float32)
-    onto = {}
-    for chunk, (begin, size) in enumerate(SHARES):
-        half = size // 2
-        to_yp, to_ym = shared[chunk]
-        if chunk > 0:
-            to_yp.wait_recv()
-            to_ym.wait_recv()
-            onto[chunk] = (across_y[chunk],)
-            continue
-        to_yp.wait_recv()
-        early = pl.ds(ym * TILES + begin, half)
-        on_yp = send(pieces.at[early], pieces.at[early], gs.at[chunk, 2], gr.at[chunk, 2], dev_yp)
-        to_ym.wait_recv()
-        late = pl.ds(yp * TILES + begin + half, half)
-        on_ym = send(pieces.at[late], pieces.at[late], gs.at[chunk, 3], gr.at[chunk, 3], dev_ym)
-        onto[chunk] = (on_yp, on_ym)
-    for chunk in range(len(SHARES)):
-        for copy in onto[chunk]:
+    for number in range(len(SHARES)):
+        for copy in shared[number] + (across_y[number],):
             copy.wait_recv()
-
     listed.wait()
 
     def choose(number, z):

time: 98.3 us -> 99.5 us (1.012)
  no operation moved by 1% of the time
where the time goes in v11:
time: 99.5 us; the launch traced here: 97.8 us
  Pallas kernels  94.9 us (95%)
  local copies, waits for them, and re-layouts  2.09 us (2%)
    pallas_call x1, Pallas kernels, gram(): pl.pallas_call(kernel, out_shape=jax.ShapeDtypeStruct((1, SLOTS, 16, BLOC...  94.9 us
    unnamed x4, local copies, waits for them, and re-layouts  2.09 us

profile of v11, /device:TPU:16, one launch (start us, length us, event | category | flops | bytes accessed | tf_op | source)
XLA Modules:
  0.0 97.8 jit_solution(6872289920697040836)
XLA Ops:
  0.0 0.0 copy-start
  0.0 1.4 %copy-done = bf16[3,256,1024]{2,1,0:T(8,128)(2,1)S(1)} copy-done((bf16[3,256,1024]{2,1,0:T(8,128)(2,1)S(1)}, bf16[3,256,1024]{2,1,0:T(8,128)(2,1)}, u32[]{:S(2)}) %copy-start) | copy-done | bytes 1572888
  1.4 0.0 copy-start.1
  1.4 0.7 copy-done.1
  2.1 94.9 %gram_tiles.1 = f32[1,20,16,256]{3,2,1,0:T(8,128)S(1)} custom-call(bf16[3,256,1024]{2,1,0:T(8,128)(2,1)S(1)} %copy-done, s32[1,2,20]{2,1,0:T(2,128)S(1)} %bitcast.1), custom_call_target="tpu_custom_call" | custom-call | tf_op jit(solution)/shard_map/gram_tiles/pallas_call | solution.py:476
  97.0 0.8 broadcast_multiply_fusion
Async XLA Ops:
  0.0 1.4 %copy-start = (bf16[3,256,1024]{2,1,0:T(8,128)(2,1)S(1)}, bf16[3,256,1024]{2,1,0:T(8,128)(2,1)}, u32[]{:S(2)}) copy-start(bf16[3,256,1024]{2,1,0:T(8,128)(2,1)} %x_ref.1) | copy-start | bytes 4718596
  1.4 0.7 copy-start.1
